TPU v7x, 128 devices: a whole 4x4x4 slice. The times are simulated.
128 devices in a mesh: gx: 8 (over z_hi, y), gy: 16 (over z_lo, x, core).
Axes of the slice: x: 4, y: 4, z: 4 (z_hi: 2, z_lo: 2; z = z_hi * 2 + z_lo), core: 2. Of those that a mesh axis runs over, the one named last changes fastest.
Arguments:
- adjoint_e: bfloat16 [3, 256, 1024, 128], P(None, 'gx', 'gy'), may hold values from -6 to 6
- adjoint_h: bfloat16 [3, 256, 1024, 128], P(None, 'gx', 'gy'), may hold values from -6 to 6
- material: int32 [256, 1024, 128], P('gx', 'gy'), may hold values from 0 to 3
- inv_eps: float32 [4], replicated, may hold values from 0.08 to 1
- forward_design: bfloat16 [3, 256, 1024, 128], P(None, 'gx', 'gy'), may hold values from -6 to 6
- cell_slot: int32 [256, 1024], P('gx', 'gy'), may hold values from 0 to 511, as said below
- tile_pillars: int32 [8, 16, 512], replicated, may hold values from -1 to 65535, as said below
- pillar_rank: int32 [65536], replicated, may hold values from 0 to 65535, as said below
Outputs:
- new_e: bfloat16 [3, 256, 1024, 128], P(None, 'gx', 'gy')
- new_h: bfloat16 [3, 256, 1024, 128], P(None, 'gx', 'gy')
- gradient: float32 [32, 65536], P(None, ('gx', 'gy'))
Inputs may be any that keep to these rules, and one draw needn't show every extreme that they name: `cell_slot`: the cell's slot holds the id of the pillar that covers the cell. `tile_pillars`: pillars are rectangles of 2 or 3 cells along x and along y that tile the lateral grid and never cross a tile's border. The lx-th pillar along x and ly-th along y of tile (tx, ty), counted from the tile's low corner, has id (tx * 16 + lx) * 512 + ty * 32 + ly. Each tile lists every pillar in it exactly once, in no particular order, with -1 in unused slots; tile (0, 0) uses all 512 slots. `pillar_rank`: A permutation of the pillar ids; rank r is owned by device r // 512 of gx+gy. Of the 512 ids of one tile, exactly 4 have ranks owned by each device.
All inputs are finite; a program needn't handle non-finite values.
Results may differ from a plain program's by a relative error of at most 0.0049.
Values may be sent and summed in bfloat16 or wider, within the bound.
No kernel may reach another device: no remote copies, remote signals or barrier semaphores. Data moves between devices by JAX's collectives and lax.ppermute only.
A program may use at most 128 MiB of HBM per device.

v0:
```python
import jax
import jax.numpy as jnp
from jax import lax
from jax.sharding import PartitionSpec as P

DL = 32


courant = 0.5
grad_scale = 0.125


def shifted(block, axis, distance):
    devices = range(lax.axis_size(axis))
    route = [(i - distance, i) for i in devices if i - distance in devices]
    return lax.ppermute(block, axis, route)


def next_cell(field, axis):
    rest = lax.slice_in_dim(field, 1, field.shape[axis], axis=axis)
    edge = jnp.zeros_like(lax.slice_in_dim(field, 0, 1, axis=axis))
    return jnp.concatenate([rest, edge], axis=axis)


def prior_cell(field, axis):
    rest = lax.slice_in_dim(field, 0, field.shape[axis] - 1, axis=axis)
    edge = jnp.zeros_like(lax.slice_in_dim(field, 0, 1, axis=axis))
    return jnp.concatenate([edge, rest], axis=axis)


def join_next(field, face, axis):
    rest = lax.slice_in_dim(field, 1, field.shape[axis], axis=axis)
    return jnp.concatenate([rest, jnp.expand_dims(face.astype(jnp.float32), axis)], axis=axis)


def join_prior(field, face, axis):
    rest = lax.slice_in_dim(field, 0, field.shape[axis] - 1, axis=axis)
    return jnp.concatenate([jnp.expand_dims(face.astype(jnp.float32), axis), rest], axis=axis)


def material_coefficient(material, inv_eps):
    coefficient = jnp.zeros(material.shape, jnp.float32)
    for which in range(inv_eps.shape[0]):
        coefficient = coefficient + jnp.where(
            material == which, inv_eps[which], jnp.zeros((), jnp.float32)
        )
    return courant * coefficient


def per_device(
    adjoint_e, adjoint_h, material, inv_eps, forward_design, cell_slot, tile_pillars, pillar_rank
):
    slot_count = tile_pillars.shape[2]
    total_pillars = pillar_rank.shape[0]
    gx_index = lax.axis_index("gx")
    gy_index = lax.axis_index("gy")
    design_depth = forward_design.shape[3]
    offset = (adjoint_e.shape[3] - design_depth) // 2
    slab = adjoint_e.astype(jnp.float32)
    intersection_density = jnp.sum(slab * forward_design.astype(jnp.float32), axis=0)
    cells_x, cells_y = cell_slot.shape
    layer_sums = intersection_density.reshape(cells_x * cells_y, DL, design_depth // DL).sum(axis=2)
    one_hot = (
        cell_slot.reshape(-1)[:, None] == jnp.arange(slot_count, dtype=jnp.int32)[None, :]
    ).astype(jnp.float32)
    partial_value = grad_scale * jnp.einsum(
        "cl,cs->ls",
        layer_sums,
        one_hot,
        precision=lax.Precision.HIGHEST,
        preferred_element_type=jnp.float32,
    )
    all_ranks = jnp.where(tile_pillars >= 0, pillar_rank[jnp.maximum(tile_pillars, 0)], -1)
    own_ranks = lax.dynamic_index_in_dim(
        lax.dynamic_index_in_dim(all_ranks, gx_index, 0, keepdims=False),
        gy_index,
        0,
        keepdims=False,
    )
    targets = jnp.where(own_ranks >= 0, own_ranks, total_pillars)
    dense_sums = (
        jnp.zeros((DL, total_pillars), jnp.float32).at[:, targets].add(partial_value, mode="drop")
    )
    gradient = lax.psum_scatter(dense_sums, ("gx", "gy"), scatter_dimension=1, tiled=True)
    faces_x = shifted((adjoint_e[1, 0], adjoint_e[2, 0]), "gx", -1)
    faces_y = shifted((adjoint_e[0, :, 0], adjoint_e[2, :, 0]), "gy", -1)
    efield_x = adjoint_e[0].astype(jnp.float32)
    efield_y = adjoint_e[1].astype(jnp.float32)
    efield_z = adjoint_e[2].astype(jnp.float32)
    hnew_x = adjoint_h[0].astype(jnp.float32) - courant * (
        join_next(efield_z, faces_y[1], 1) - efield_z - (next_cell(efield_y, 2) - efield_y)
    )
    hnew_y = adjoint_h[1].astype(jnp.float32) - courant * (
        next_cell(efield_x, 2) - efield_x - (join_next(efield_z, faces_x[1], 0) - efield_z)
    )
    hnew_z = adjoint_h[2].astype(jnp.float32) - courant * (
        join_next(efield_y, faces_x[0], 0)
        - efield_y
        - (join_next(efield_x, faces_y[0], 1) - efield_x)
    )
    new_h = jnp.stack([hnew_x, hnew_y, hnew_z]).astype(jnp.bfloat16)
    back_x = shifted((new_h[1, -1], new_h[2, -1]), "gx", 1)
    back_y = shifted((new_h[0, :, -1], new_h[2, :, -1]), "gy", 1)
    magnetic_x = new_h[0].astype(jnp.float32)
    magnetic_y = new_h[1].astype(jnp.float32)
    magnetic_z = new_h[2].astype(jnp.float32)
    coefficient = material_coefficient(material, inv_eps)
    enew_x = efield_x + coefficient * (
        magnetic_z - join_prior(magnetic_z, back_y[1], 1) - (magnetic_y - prior_cell(magnetic_y, 2))
    )
    enew_y = efield_y + coefficient * (
        magnetic_x - prior_cell(magnetic_x, 2) - (magnetic_z - join_prior(magnetic_z, back_x[1], 0))
    )
    enew_z = efield_z + coefficient * (
        magnetic_y
        - join_prior(magnetic_y, back_x[0], 0)
        - (magnetic_x - join_prior(magnetic_x, back_y[0], 1))
    )
    new_e = jnp.stack([enew_x, enew_y, enew_z]).astype(jnp.bfloat16)
    return (new_e, new_h, gradient)


def solution(mesh):
    return jax.shard_map(
        per_device,
        mesh=mesh,
        in_specs=(
            P(None, "gx", "gy", None),
            P(None, "gx", "gy", None),
            P("gx", "gy", None),
            P(),
            P(None, "gx", "gy", None),
            P("gx", "gy"),
            P(),
            P(),
        ),
        out_specs=(P(None, "gx", "gy", None), P(None, "gx", "gy", None), P(None, ("gx", "gy"))),
        check_vma=False,
    )
```

profile of v0, /device:TPU:0, one launch (start us, length us, event | category | flops | bytes accessed | tf_op | source)
XLA Modules:
  0.0 1105.3 jit_solution(11041758536205654177)
XLA Ops:
  7.2 0.0 copy-start
  7.2 0.0 reduce-scatter.2.cloned.1.call-start
  7.2 0.8 eq.47
  8.1 1.0 broadcast_maximum_fusion
  9.0 0.1 copy.80
  9.2 0.0 copy-start.2
  9.2 362.7 %gather_fusion = s32[65536]{0:T(1024)S(1)} fusion(s32[65536]{0:T(1024)S(1)} %copy-done, s32[65536]{0:T(1024)S(1)} %broadcast_clamp_fusion), kind=kCustom, calls=%fused_computation | custom fusion | bytes 786432 | tf_op jit(solution)/shard_map/gather | solution.py:73
  371.9 2.1 multiply_reduce_fusion
  374.1 1.8 copy.65
  375.9 0.8 reshape.66
  376.7 0.6 reduce_sum.19
  377.4 1.6 fusion.5
  379.0 0.1 copy.66
  379.1 0.7 compare_select_fusion
  379.9 15.4 %scatter_custom_fusion = f32[32,65536]{0,1:T(8,128)} fusion(s32[512]{0:T(512)S(1)} %bitcast.137, f32[512,32]{1,0:T(8,128)S(1)} %copy.66, f32[]{:T(128)} %constant.47.clone.1), kind=kCustom, calls=%fused_computation.2 | custom fusion | flops 16384 | bytes 8388612 | tf_op jit(solution)/shard_map/scatter-add | solution.py:82
  395.3 0.0 reduce-scatter.2.cloned.1.call-update
  395.3 1.4 copy-done.3
  396.8 1.3 collective-permute-start.4
  398.1 1.3 collective-permute-start.1
  399.4 1.3 collective-permute-start
  400.7 1.3 collective-permute-start.3
  402.0 0.1 fusion.41
  402.1 0.0 copy-start.5
  402.1 0.3 convert_bitcast_fusion
  402.4 0.1 slice_bitcast_fusion.3
  402.5 1.0 copy-done.5
  403.5 0.1 fusion.39
  403.6 0.7 copy_convert_fusion
  404.3 0.0 copy-start.6
  404.3 0.1 slice_bitcast_fusion.2
  404.5 0.5 copy-done.6
  405.0 0.7 fusion.42
  405.7 0.3 slice.149
  406.0 0.1 slice.145
  406.1 0.1 slice.152
  406.2 0.3 slice.153
  406.6 0.0 collective-permute-done.4
  406.6 0.0 collective-permute-done.1
  406.6 0.0 collective-permute-done
  406.6 1.1 convert_bitcast_fusion.2
  407.7 0.1 convert_element_type.78
  407.9 0.0 collective-permute-done.3
  407.9 2.0 convert_bitcast_fusion.1
  410.0 0.1 convert_element_type.84
  410.1 0.1 slice.160
  410.2 0.1 slice.154
  410.4 0.1 slice.148
  410.5 3.7 collective-permute-start.2
  414.1 4.9 collective-permute-start.5
  419.1 3.8 collective-permute-start.7
  422.9 4.0 collective-permute-start.6
  426.9 0.1 slice_bitcast_fusion.1
  427.0 0.1 slice_bitcast_fusion
  427.1 0.2 pad_maximum_fusion.1
  427.3 0.0 copy-start.4
  427.3 1.8 copy.68
  429.0 0.0 collective-permute-done.2
  429.1 4.0 fusion.33
  433.1 4.4 fusion.31
  437.6 0.0 copy-start.1
  437.6 0.2 pad_maximum_fusion
  437.7 1.8 copy.67
  439.5 657.3 %reduce-scatter.2.cloned.1.call-done = f32[32,512]{0,1:T(8,128)} async-done(((f32[32,65536]{0,1:T(8,128)}), f32[32,512]{0,1:T(8,128)}) %reduce-scatter.2.cloned.1.call-update) | async-done | bytes 65552 | tf_op jit(solution)/shard_map/reduce_scatter | solution.py:84
  1096.8 1.7 copy.69
  (28 shorter events, 0.3 us)
Async XLA Ops:
  7.2 2.0 copy-start
  7.2 1089.6 %reduce-scatter.2.cloned.1.call-start = ((), (), s32[]{:S(2)}) async-start(), calls=%async_computation.1 | async-start | bytes 33816576 | tf_op jit(solution)/shard_map/reduce_scatter | solution.py:84
  9.2 362.8 %copy-start.2 = (bf16[3,32,64,128]{3,2,1,0:T(8,128)(2,1)S(1)}, bf16[3,32,64,128]{3,2,1,0:T(8,128)(2,1)}, u32[]{:S(2)}) copy-start(bf16[3,32,64,128]{3,2,1,0:T(8,128)(2,1)} %param.8) | copy-start | bytes 4718596
  395.3 1.4 copy-start.3
  396.8 9.8 collective-permute-start.4
  398.1 8.5 collective-permute-start.1
  399.4 7.2 collective-permute-start
  400.7 7.2 collective-permute-start.3
  402.1 1.4 copy-start.5
  404.3 0.7 copy-start.6
  410.5 18.6 %collective-permute-start.2 = (bf16[32,128]{1,0:T(8,128)(2,1)S(1)}, bf16[32,128]{1,0:T(8,128)(2,1)S(1)}, u32[]{:S(2)}, u32[]{:S(2)}) collective-permute-start(bf16[32,128]{1,0:T(8,128)(2,1)S(1)} %slice_bitcast_fusion.7), channel_id=1, source_target_pairs={{0,1},{1,2},{2,3},{3,4},{4,5},{5,6},{6,7},{7,8},{8,9},{9,10},{10,1... | collective-permute-start | bytes 24584 | tf_op jit(solution)/shard_map/ppermute | solution.py:16
  414.1 14.9 %collective-permute-start.5 = (bf16[64,128]{1,0:T(8,128)(2,1)S(1)}, bf16[64,128]{1,0:T(8,128)(2,1)S(1)}, u32[]{:S(2)}, u32[]{:S(2)}) collective-permute-start(bf16[64,128]{1,0:T(8,128)(2,1)S(1)} %bitcast.133), channel_id=1, source_target_pairs={{0,16},{16,32},{32,48},{48,64},{64,80},{80,96},{96,112},{1,17},{17... | collective-permute-start | bytes 49160 | tf_op jit(solution)/shard_map/ppermute | solution.py:16
  419.1 10.0 collective-permute-start.7
  422.9 6.2 collective-permute-start.6
  427.3 1.8 copy-start.4
  437.6 660.9 %copy-start.1 = (s32[65536]{0:T(1024)S(1)}, s32[65536]{0:T(1024)}, u32[]{:S(2)}) copy-start(s32[65536]{0:T(1024)} %param.15) | copy-start | bytes 786436
Sparse Core Ops, SparseCore 0:
  395.4 701.2 reduce-scatter.1
where the time goes:
time: 1110 us
  waiting for transfers between devices  657 us (59%)
  local copies, waits for them, and re-layouts  377 us (34%)
  other arithmetic  33.1 us (3%)
  starting transfers between devices  21.6 us (2%)
  between operations  14.6 us (1%)
    reduce_scatter x1, waiting for transfers between devices, per_device(): lax.psum_scatter(dense_sums, ('gx', 'gy'), scatter_dimension=1, tiled=True)  657 us
    gather x2, local copies, waits for them, and re-layouts, per_device(): pillar_rank[jnp.maximum(tile_pillars, 0)]  363 us
  transfers between devices with their start and end apart: 9, of which 1 were waited for; matrix products, arithmetic and copies ran while one was open for 2% of the time, Pallas kernels for 0%

commit v1 on v0

v1 whole, which is shorter than its diff:
```python
import jax
import jax.numpy as jnp
from jax import lax
from jax.experimental import pallas as pl
from jax.experimental.pallas import tpu as pltpu
from jax.sharding import PartitionSpec as P

F32, BF16, I32 = jnp.float32, jnp.bfloat16, jnp.int32
ANY = pl.BlockSpec(memory_space=pl.ANY)
VM = pl.BlockSpec(memory_space=pltpu.VMEM)
SM = pl.BlockSpec(memory_space=pltpu.SMEM)
DL = 32
CHUNKS = 8


def split(v):
    hi = v.astype(BF16)
    return hi, (v - hi.astype(F32)).astype(BF16)


def iota(shape, axis):
    return lax.broadcasted_iota(I32, shape, axis)


def dot(a, b):
    return jnp.dot(a, b, preferred_element_type=F32)


def pillar_kernel(
    e_hbm, h_hbm, f_hbm, slot_ref, tiles_hbm, rank_hbm,
    send_ref, xa_ref, xb_ref, ya_ref, yb_ref, c_ref, d_ref, y0_ref,
    e, f, hx, hy, tiles, rank, cells, acc, sem, fsem, msem,
):
    gx, gy = lax.axis_index("gx"), lax.axis_index("gy")
    _, nx, ny, nz = e.shape
    step = nx // CHUNKS
    copies = []
    for i in range(CHUNKS):
        part = pl.ds(i * step, step)
        copies.append((
            pltpu.make_async_copy(e_hbm.at[:, part], e.at[:, part], sem.at[i]),
            pltpu.make_async_copy(f_hbm.at[:, part], f.at[:, part], fsem.at[i]),
        ))
    extra = [
        pltpu.make_async_copy(tiles_hbm.at[gx, pl.ds(gy // 8 * 8, 8)], tiles, msem.at[0]),
        pltpu.make_async_copy(rank_hbm.at[pl.ds(gx * 64, 64)], rank, msem.at[1]),
        pltpu.make_async_copy(h_hbm.at[pl.ds(1, 2), nx - 1], hx, msem.at[2]),
        pltpu.make_async_copy(h_hbm.at[0, :, pl.ds(ny - 8, 8)], hy.at[0], msem.at[3]),
        pltpu.make_async_copy(h_hbm.at[2, :, pl.ds(ny - 8, 8)], hy.at[1], msem.at[4]),
    ]
    for one, two in copies[:1]:
        one.start()
        two.start()
    for one in extra:
        one.start()
    for one, two in copies[1:]:
        one.start()
        two.start()

    cells[:, :ny] = slot_ref[...]
    cells[:, ny:] = slot_ref[...]
    half = nx // 2
    lane = iota((half, 2 * ny), 1)
    pair = jnp.where(lane < ny, cells[pl.ds(0, half, stride=2), :], cells[pl.ds(1, half, stride=2), :])

    extra[0].wait()
    extra[1].wait()
    own = jnp.sum(jnp.where(iota(tiles.shape, 0) == gy % 8, tiles[...], 0), axis=0, keepdims=True)
    along_x = own // 512 - gx * 16
    along_y = own % 512 - gy * 32
    quarter = gy // 4
    ranks = jnp.zeros((16, 128), I32)
    for q in range(4):
        ranks = jnp.where(quarter == q, rank[pl.ds(q, 16, stride=4), :], ranks)
    turned = ranks
    for q in range(1, 4):
        turned = jnp.where(gy % 4 == q, pltpu.roll(ranks, 128 - 32 * q, 1), turned)
    square = jnp.concatenate([turned, jnp.zeros((112, 128), I32)], axis=0)
    columns = jnp.transpose(square)[:32]
    slots = own.shape[1]
    found = jnp.zeros((32, slots), I32)
    for q in range(16):
        found = jnp.where(along_x == q, columns[:, q : q + 1], found)
    my_rank = jnp.sum(jnp.where(iota((32, slots), 0) == along_y, found, 0), axis=0, keepdims=True)
    below = jnp.zeros((32, slots), I32)
    for q in range(16):
        below = below + jnp.where(columns[:, q : q + 1] < my_rank, 1, 0)
    order = jnp.sum(below, axis=0, keepdims=True)
    row = jnp.where(own >= 0, (order & 3) * 128 + (order >> 2), -1)
    place = (my_rank & 511).astype(F32)

    acc[...] = jnp.zeros(acc.shape, F32)
    for i, (one, two) in enumerate(copies):
        one.wait()
        two.wait()
        part = pl.ds(i * step, step)
        density = jnp.zeros((step * ny, nz), F32)
        for c in range(3):
            density = density + (
                e[c, part].astype(F32) * f[c, part].astype(F32)
            ).reshape(step * ny, nz)
        hi, lo = split(density)
        both = jnp.concatenate([hi, lo], axis=1)
        hot = jnp.concatenate(
            [
                jnp.where(iota((slots, 128), 0) == pair[p : p + 1], 1.0, 0.0).astype(BF16)
                for p in range(i * step // 2, (i + 1) * step // 2)
            ],
            axis=1,
        )
        acc[...] += dot(hot, both)

    sums = acc[:, :nz] + acc[:, nz:]
    hi, lo = split(sums)
    match = iota((slots, slots), 0) == row
    moved = dot(jnp.where(match, 1.0, 0.0).astype(BF16), jnp.concatenate([hi, lo], axis=1))
    moved = moved[:, :nz] + moved[:, nz:]
    spot = jnp.sum(jnp.where(match, place, 0.0), axis=1, keepdims=True)
    lanes = iota((128, 128), 1)
    values, spots = jnp.zeros((128, 128), F32), jnp.zeros((128, 128), F32)
    for k in range(4):
        hi, lo = split(moved[k * 128 : (k + 1) * 128])
        gather = jnp.where(lanes == 32 * k + iota((128, 128), 0) // 4, 0.125, 0.0).astype(BF16)
        values = values + dot(hi, gather) + dot(lo, gather)
        spots = jnp.where(lanes == k, spot[k * 128 : (k + 1) * 128], spots)
    send_ref[pl.ds(0, 128, stride=2), :] = values
    send_ref[pl.ds(1, 128, stride=2), :] = spots

    for one in extra[2:]:
        one.wait()

    def face(c, y):
        base = y // 8 * 8
        return e[c, :, pl.ds(base, 8), :].astype(F32)[:, y - base, :]

    y0x, y0z, y0y = face(0, 0), face(2, 0), None
    y0_ref[0] = y0x
    y0_ref[1] = y0z
    last = ny - 1
    up_y = [face(0, last), face(1, last), face(2, last)]
    up_y += [hy[0].astype(F32)[:, 7, :], hy[1].astype(F32)[:, 7, :]]

    def pack_x(up_ref, down_ref):
        for c in range(3):
            up_ref[c] = e[c, nx - 1]
        up_ref[3] = hx[0]
        up_ref[4] = hx[1]
        down_ref[0] = e[1, 0]
        down_ref[1] = e[2, 0]
        for c in range(2, 5):
            down_ref[c] = jnp.zeros((ny, nz), BF16)

    def pack_y(up_ref, down_ref):
        for c in range(5):
            up_ref[c] = up_y[c].astype(BF16)
        down_ref[0] = y0x.astype(BF16)
        down_ref[1] = y0z.astype(BF16)
        for c in range(2, 5):
            down_ref[c] = jnp.zeros((nx, nz), BF16)

    def pack_corner(up_ref, down_ref):
        up_ref[...] = jnp.broadcast_to(y0x[nx - 1 : nx], (8, nz))
        down_ref[...] = jnp.broadcast_to(up_y[1][0:1], (8, nz))

    @pl.when(gx % 2 == 0)
    def _():
        pack_x(xa_ref, xb_ref)
        pack_corner(c_ref, d_ref)

    @pl.when(gx % 2 == 1)
    def _():
        pack_x(xb_ref, xa_ref)
        pack_corner(d_ref, c_ref)

    @pl.when(gy % 2 == 0)
    def _():
        pack_y(ya_ref, yb_ref)

    @pl.when(gy % 2 == 1)
    def _():
        pack_y(yb_ref, ya_ref)


def field_kernel(
    e_hbm, h_hbm, m_hbm, eps_ref, xa_ref, xb_ref, ya_ref, yb_ref, c_ref, d_ref, y0_ref,
    ne_hbm, nh_hbm,
    e, h, m, ne, nh, yup, ylow, sem, hsem, msem, esem, osem,
):
    gx, gy = lax.axis_index("gx"), lax.axis_index("gy")
    _, nx, ny, nz = h.shape
    step = nx // CHUNKS
    loads = []
    for i in range(CHUNKS):
        part = pl.ds(i * step, step)
        loads.append((
            pltpu.make_async_copy(e_hbm.at[:, part], e.at[:, part], sem.at[i]),
            pltpu.make_async_copy(h_hbm.at[:, part], h.at[:, part], hsem.at[i]),
            pltpu.make_async_copy(m_hbm.at[part], m.at[part], msem.at[i]),
        ))
    for group in loads:
        for one in group:
            one.start()
    stores = []
    for i in range(CHUNKS):
        part = pl.ds(i * step, step)
        stores.append((
            pltpu.make_async_copy(nh.at[:, part], nh_hbm.at[:, part], osem.at[i]),
            pltpu.make_async_copy(ne.at[:, part], ne_hbm.at[:, part], esem.at[i]),
        ))

    even_x, even_y = gx % 2 == 0, gy % 2 == 0
    last_lane = iota((ny, nz), 1) == nz - 1
    first_lane = iota((ny, nz), 1) == 0
    last_row = iota((ny, nz), 0) == ny - 1
    first_row = iota((ny, nz), 0) == 0

    def up_z(v):
        return jnp.where(iota(v.shape, 1) == nz - 1, 0.0, pltpu.roll(v, nz - 1, 1))

    def low_z(v):
        return jnp.where(iota(v.shape, 1) == 0, 0.0, pltpu.roll(v, 1, 1))

    def up_y(v, edge):
        n = v.shape[0]
        return jnp.where(iota(v.shape, 0) == n - 1, edge, pltpu.roll(v, n - 1, 0))

    def low_y(v, edge):
        return jnp.where(iota(v.shape, 0) == 0, edge, pltpu.roll(v, 1, 0))

    def either(flag, a, b):
        return jnp.where(flag, a.astype(F32), b.astype(F32))

    for c in range(2):
        e[c + 1, nx] = either(even_x, xa_ref[c], xb_ref[c]).astype(BF16)
        yup[c] = either(even_y, ya_ref[c], yb_ref[c])
    ly = [either(even_y, yb_ref[c], ya_ref[c]) for c in range(5)]
    edge = jnp.where(even_x, c_ref[0:1], d_ref[0:1])
    inside = jnp.where(gy > 0, 1.0, 0.0)
    ex, ey, ez, hx, hz = ly
    ylow[0] = (inside * (hx - 0.5 * ((y0_ref[1] - ez) - (up_z(ey) - ey)))).astype(BF16).astype(F32)
    ylow[1] = (inside * (hz - 0.5 * ((up_y(ey, edge) - ey) - (y0_ref[0] - ex)))).astype(BF16).astype(F32)
    for one in loads[0]:
        one.wait()
    ex, ey, ez, hy, hz = [either(even_x, xb_ref[c], xa_ref[c]) for c in range(5)]
    edge = jnp.where(even_x, d_ref[0:1], c_ref[0:1])
    inside = jnp.where(gx > 0, 1.0, 0.0)
    e0y, e0z = e[1, 0].astype(F32), e[2, 0].astype(F32)
    hy_low = (inside * (hy - 0.5 * ((up_z(ex) - ex) - (e0z - ez)))).astype(BF16)
    hz_low = (inside * (hz - 0.5 * ((e0y - ey) - (up_y(ex, edge) - ex)))).astype(BF16)

    coefs = [0.5 * eps_ref[k] for k in range(4)]

    def plane(x, carry):
        hy_low, hz_low = carry
        ex, ey, ez = [e[c, x].astype(F32) for c in range(3)]
        eyn, ezn = e[1, x + 1].astype(F32), e[2, x + 1].astype(F32)
        upx, upz = yup[0, pl.ds(x, 1)], yup[1, pl.ds(x, 1)]
        bx = (h[0, x].astype(F32) - 0.5 * ((up_y(ez, upz) - ez) - (up_z(ey) - ey))).astype(BF16)
        by = (h[1, x].astype(F32) - 0.5 * ((up_z(ex) - ex) - (ezn - ez))).astype(BF16)
        bz = (h[2, x].astype(F32) - 0.5 * ((eyn - ey) - (up_y(ex, upx) - ex))).astype(BF16)
        nh[0, x] = bx
        nh[1, x] = by
        nh[2, x] = bz
        hx, hy, hz = bx.astype(F32), by.astype(F32), bz.astype(F32)
        mat = m[x]
        coef = jnp.where(mat == 0, coefs[0], jnp.where(mat == 1, coefs[1], jnp.where(mat == 2, coefs[2], coefs[3])))
        lowx, lowz = ylow[0, pl.ds(x, 1)], ylow[1, pl.ds(x, 1)]
        ne[0, x] = (ex + coef * ((hz - low_y(hz, lowz)) - (hy - low_z(hy)))).astype(BF16)
        ne[1, x] = (ey + coef * ((hx - low_z(hx)) - (hz - hz_low.astype(F32)))).astype(BF16)
        ne[2, x] = (ez + coef * ((hy - hy_low.astype(F32)) - (hx - low_y(hx, lowx)))).astype(BF16)
        return by, bz

    carry = (hy_low, hz_low)
    for i in range(CHUNKS):
        if i + 1 < CHUNKS:
            for one in loads[i + 1]:
                one.wait()
        carry = lax.fori_loop(i * step, (i + 1) * step, plane, carry)
        for one in stores[i]:
            one.start()
    for group in stores:
        for one in group:
            one.wait()


def place_kernel(got_ref, grad_ref):
    values = jnp.transpose(got_ref[pl.ds(0, 128, stride=2), :])
    spots = got_ref[pl.ds(1, 128, stride=2), :].astype(I32)
    ranks = grad_ref.shape[1]
    total = jnp.zeros((2 * DL, ranks), F32)
    for k in range(4):
        hot = jnp.where(iota((128, ranks), 1) == spots[:, k : k + 1], 1.0, 0.0).astype(BF16)
        hi, lo = split(values[k * DL : (k + 1) * DL])
        total = total + dot(jnp.concatenate([hi, lo], axis=0), hot)
    grad_ref[...] = total[:DL] + total[DL:]


def per_device(
    adjoint_e, adjoint_h, material, inv_eps, forward_design, cell_slot, tile_pillars, pillar_rank
):
    _, nx, ny, nz = adjoint_e.shape
    sx, sy = lax.axis_size("gx"), lax.axis_size("gy")
    both = ("gx", "gy")
    params = pltpu.CompilerParams(vmem_limit_bytes=40 * 1024 * 1024)
    shape = jax.ShapeDtypeStruct
    send, xa, xb, ya, yb, c, d, y0 = pl.pallas_call(
        pillar_kernel,
        out_shape=(
            shape((256, 128), F32),
            shape((5, ny, nz), BF16), shape((5, ny, nz), BF16),
            shape((5, nx, nz), BF16), shape((5, nx, nz), BF16),
            shape((8, nz), F32), shape((8, nz), F32),
            shape((2, nx, nz), F32),
        ),
        in_specs=[ANY, ANY, ANY, VM, ANY, ANY],
        out_specs=[VM] * 8,
        scratch_shapes=[
            pltpu.VMEM((3, nx, ny, nz), BF16), pltpu.VMEM((3, nx, ny, nz), BF16),
            pltpu.VMEM((2, ny, nz), BF16), pltpu.VMEM((2, nx, 8, nz), BF16),
            pltpu.VMEM((8, 512), I32), pltpu.VMEM((64, 128), I32),
            pltpu.VMEM((nx, 2 * ny), I32), pltpu.VMEM((512, 2 * nz), F32),
            pltpu.SemaphoreType.DMA((CHUNKS,)), pltpu.SemaphoreType.DMA((CHUNKS,)),
            pltpu.SemaphoreType.DMA((5,)),
        ],
        compiler_params=params,
        name="pillars",
    )(adjoint_e, adjoint_h, forward_design, cell_slot, tile_pillars, pillar_rank.reshape(512, 128))

    got = lax.all_to_all(send.reshape(128, 2, 128), both, 0, 0, tiled=True).reshape(256, 128)

    def swap(v, axis, size, low):
        pairs = []
        for i in range(low, size - 1, 2):
            pairs += [(i, i + 1), (i + 1, i)]
        return lax.ppermute(v, axis, pairs)

    def swap_corner(v, low):
        pairs = []
        for i in range(low, sx - 1, 2):
            for j in range(1, sy):
                one, two = i * sy + j, (i + 1) * sy + j - 1
                pairs += [(one, two), (two, one)]
        return lax.ppermute(v, both, pairs)

    xa, xb = swap(xa, "gx", sx, 0), swap(xb, "gx", sx, 1)
    ya, yb = swap(ya, "gy", sy, 0), swap(yb, "gy", sy, 1)
    c, d = swap_corner(c, 0), swap_corner(d, 1)

    new_e, new_h = pl.pallas_call(
        field_kernel,
        out_shape=(shape(adjoint_e.shape, BF16), shape(adjoint_e.shape, BF16)),
        in_specs=[ANY, ANY, ANY, SM] + [VM] * 7,
        out_specs=[ANY, ANY],
        scratch_shapes=[
            pltpu.VMEM((3, nx + 1, ny, nz), BF16), pltpu.VMEM((3, nx, ny, nz), BF16),
            pltpu.VMEM((nx, ny, nz), I32),
            pltpu.VMEM((3, nx, ny, nz), BF16), pltpu.VMEM((3, nx, ny, nz), BF16),
            pltpu.VMEM((2, nx, nz), F32), pltpu.VMEM((2, nx, nz), F32),
        ] + [pltpu.SemaphoreType.DMA((CHUNKS,))] * 5,
        compiler_params=params,
        name="fields",
    )(adjoint_e, adjoint_h, material, inv_eps, xa, xb, ya, yb, c, d, y0)

    gradient = pl.pallas_call(
        place_kernel,
        out_shape=shape((DL, 512), F32),
        in_specs=[VM],
        out_specs=VM,
        compiler_params=params,
        name="place",
    )(got)
    return new_e, new_h, gradient


def solution(mesh):
    return jax.shard_map(
        per_device,
        mesh=mesh,
        in_specs=(
            P(None, "gx", "gy", None),
            P(None, "gx", "gy", None),
            P("gx", "gy", None),
            P(),
            P(None, "gx", "gy", None),
            P("gx", "gy"),
            P(),
            P(),
        ),
        out_specs=(P(None, "gx", "gy", None), P(None, "gx", "gy", None), P(None, ("gx", "gy"))),
        check_vma=False,
    )
```

time: 1110 us -> 63 us (0.06)
  the two profiles are of different devices: /device:TPU:0 before, /device:TPU:31 now
where the time goes in v1:
time: 63 us; the launch traced here: 62.6 us
  starting transfers between devices  24 us (38%)
  Pallas kernels  16.6 us (26%)
  waiting for transfers between devices  12.6 us (20%)
  local copies, waits for them, and re-layouts  8.67 us (14%)
  between operations  0.77 us (1%)
    ppermute x2, waiting for transfers between devices, swap_corner(): return lax.ppermute(v, both, pairs)  12.5 us
    all_to_all x1, starting transfers between devices, per_device(): lax.all_to_all(send.reshape(128, 2, 128), both, 0, 0, tiled=True)  10.5 us
    pallas_call x1, Pallas kernels, per_device(): pl.pallas_call(field_kernel, out_shape=(shape(adjoint_e.shape, BF16), sha...  10.2 us
    ppermute x4, starting transfers between devices, swap(): return lax.ppermute(v, axis, pairs)  9.58 us
    unnamed x22, local copies, waits for them, and re-layouts  8.67 us
    pallas_call x1, Pallas kernels, per_device(): pl.pallas_call(pillar_kernel, out_shape=(shape((256, 128), F32), shape((5...  5.41 us
    ppermute x2, starting transfers between devices, swap_corner(): return lax.ppermute(v, both, pairs)  3.9 us
  transfers between devices with their start and end apart: 7, of which 2 were waited for; matrix products, arithmetic and copies ran while one was open for 0% of the time, Pallas kernels for 16%

profile of v1, /device:TPU:31, one launch (start us, length us, event | category | flops | bytes accessed | tf_op | source)
XLA Modules:
  0.0 62.6 jit_solution(7801000399994335840)
XLA Ops:
  0.6 0.0 copy-start
  0.6 1.4 %copy-done = bf16[3,32,64,128]{3,2,1,0:T(8,128)(2,1)S(1)} copy-done((bf16[3,32,64,128]{3,2,1,0:T(8,128)(2,1)S(1)}, bf16[3,32,64,128]{3,2,1,0:T(8,128)(2,1)}, u32[]{:S(2)}) %copy-start) | copy-done | bytes 1572888
  2.0 0.0 copy-start.2
  2.0 1.4 %copy-done.2 = bf16[3,32,64,128]{3,2,1,0:T(8,128)(2,1)S(1)} copy-done((bf16[3,32,64,128]{3,2,1,0:T(8,128)(2,1)S(1)}, bf16[3,32,64,128]{3,2,1,0:T(8,128)(2,1)}, u32[]{:S(2)}) %copy-start.2) | copy-done | bytes 1572888
  3.5 0.0 copy-start.4
  3.5 1.4 %copy-done.4 = bf16[3,32,64,128]{3,2,1,0:T(8,128)(2,1)S(1)} copy-done((bf16[3,32,64,128]{3,2,1,0:T(8,128)(2,1)S(1)}, bf16[3,32,64,128]{3,2,1,0:T(8,128)(2,1)}, u32[]{:S(2)}) %copy-start.4) | copy-done | bytes 1572888
  4.9 0.0 copy-start.6
  4.9 0.9 %copy-done.6 = s32[8,16,512]{2,1,0:T(8,128)S(1)} copy-done((s32[8,16,512]{2,1,0:T(8,128)S(1)}, s32[8,16,512]{2,1,0:T(8,128)}, u32[]{:S(2)}) %copy-start.6) | copy-done | bytes 262168
  5.8 0.0 copy-start.7
  5.8 0.9 %copy-done.7 = s32[65536]{0:T(1024)S(1)} copy-done((s32[65536]{0:T(1024)S(1)}, s32[65536]{0:T(1024)}, u32[]{:S(2)}) %copy-start.7) | copy-done | bytes 262168
  6.8 0.0 copy-start.8
  6.8 0.7 %copy-done.8 = s32[32,64]{1,0:T(8,128)S(1)} copy-done((s32[32,64]{1,0:T(8,128)S(1)}, s32[32,64]{1,0:T(8,128)}, u32[]{:S(2)}) %copy-start.8) | copy-done | bytes 8216
  7.5 0.0 copy-start.1
  7.5 0.0 copy-start.3
  7.5 0.0 copy-start.9
  7.5 5.4 %pillars.1 = (f32[256,128]{1,0:T(8,128)}, bf16[5,64,128]{2,1,0:T(8,128)(2,1)S(1)}, bf16[5,64,128]{2,1,0:T(8,128)(2,1)S(1)}, bf16[5,32,128]{2,1,0:T(8,128)(2,1)S(...) custom-call(bf16[3,32,64,128]{3,2,1,0:T(8,128)(2,1)S(1)} %copy-done,, ...), custom_call_target="tpu_custom_call" | custom-call | tf_op jit(solution)/shard_map/pillars/pallas_call | solution.py:306
  12.9 0.0 copy-start.10
  12.9 0.6 copy-done.10
  13.5 10.5 %all-to-all-start = ((f32[128,2,128]{2,1,0:T(2,128)}), f32[128,2,128]{2,1,0:T(2,128)S(1)}, u32[]{:S(2)}, u32[]{:S(2)}) async-start(f32[128,2,128]{2,1,0:T(2,128)} %bitcast.1), calls=%async_computation | async-start | bytes 262144 | tf_op jit(solution)/shard_map/all_to_all | solution.py:329
  24.1 0.6 collective-permute-start
  24.6 5.7 %collective-permute-start.1 = (bf16[5,64,128]{2,1,0:T(8,128)(2,1)S(1)}, bf16[5,64,128]{2,1,0:T(8,128)(2,1)S(1)}, u32[]{:S(2)}, u32[]{:S(2)}) collective-permute-start(bf16[5,64,128]{2,1,0:T(8,128)(2,1)S(1)} %get-tuple-element.14), channel_id=1, source_target_pairs={{16,32},{32,16},{48,64},{64,48},{80,96},{96,80},{17,33},{33,17},{4... | collective-permute-start | bytes 245768 | tf_op jit(solution)/shard_map/ppermute | solution.py:335
  30.3 1.0 %collective-permute-start.2 = (bf16[5,32,128]{2,1,0:T(8,128)(2,1)}, bf16[5,32,128]{2,1,0:T(8,128)(2,1)S(1)}, u32[]{:S(2)}, u32[]{:S(2)}) collective-permute-start(bf16[5,32,128]{2,1,0:T(8,128)(2,1)} %copy-done.10), channel_id=1, source_target_pairs={{0,1},{1,0},{2,3},{3,2},{4,5},{5,4},{6,7},{7,6},{8,9},{9,8},{10,11... | collective-permute-start | bytes 122888 | tf_op jit(solution)/shard_map/ppermute | solution.py:335
  31.3 2.3 %collective-permute-start.3 = (bf16[5,32,128]{2,1,0:T(8,128)(2,1)S(1)}, bf16[5,32,128]{2,1,0:T(8,128)(2,1)S(1)}, u32[]{:S(2)}, u32[]{:S(2)}) collective-permute-start(bf16[5,32,128]{2,1,0:T(8,128)(2,1)S(1)} %get-tuple-element.16), channel_id=1, source_target_pairs={{1,2},{2,1},{3,4},{4,3},{5,6},{6,5},{7,8},{8,7},{9,10},{10,9},{11,... | collective-permute-start | bytes 122888 | tf_op jit(solution)/shard_map/ppermute | solution.py:335
  33.7 2.0 %collective-permute-start.4 = (f32[8,128]{1,0:T(8,128)S(1)}, f32[8,128]{1,0:T(8,128)S(1)}, u32[]{:S(2)}, u32[]{:S(2)}) collective-permute-start(f32[8,128]{1,0:T(8,128)S(1)} %get-tuple-element.17), channel_id=1, source_target_pairs={{1,16},{16,1},{2,17},{17,2},{3,18},{18,3},{4,19},{19,4},{5,20},{20... | collective-permute-start | bytes 12296 | tf_op jit(solution)/shard_map/ppermute | solution.py:343
  35.7 5.9 %collective-permute-done.4.c_ref = f32[8,128]{1,0:T(8,128)S(1)} collective-permute-done((f32[8,128]{1,0:T(8,128)S(1)}, f32[8,128]{1,0:T(8,128)S(1)}, u32[]{:S(2)}, u32[]{:S(2)}) %collective-permute-start.4) | collective-permute-done | bytes 4128 | tf_op jit(solution)/shard_map/ppermute | solution.py:343
  41.6 1.9 %collective-permute-start.5 = (f32[8,128]{1,0:T(8,128)S(1)}, f32[8,128]{1,0:T(8,128)S(1)}, u32[]{:S(2)}, u32[]{:S(2)}) collective-permute-start(f32[8,128]{1,0:T(8,128)S(1)} %get-tuple-element.18), channel_id=1, source_target_pairs={{17,32},{32,17},{18,33},{33,18},{19,34},{34,19},{20,35},{35,20},{2... | collective-permute-start | bytes 12296 | tf_op jit(solution)/shard_map/ppermute | solution.py:343
  43.5 6.6 %collective-permute-done.5.d_ref = f32[8,128]{1,0:T(8,128)S(1)} collective-permute-done((f32[8,128]{1,0:T(8,128)S(1)}, f32[8,128]{1,0:T(8,128)S(1)}, u32[]{:S(2)}, u32[]{:S(2)}) %collective-permute-start.5) | collective-permute-done | bytes 4128 | tf_op jit(solution)/shard_map/ppermute | solution.py:343
  50.1 0.0 collective-permute-done.2.ya_ref
  50.1 0.0 collective-permute-done.3.yb_ref
  50.1 0.0 collective-permute-done.xa_ref
  50.1 0.0 collective-permute-done.1.xb_ref
  50.1 0.0 copy-done.1
  50.2 0.0 copy-done.3
  50.2 0.0 copy-done.9
  50.2 0.0 copy-start.5
  50.2 1.2 %copy-done.5 = s32[32,64,128]{2,1,0:T(8,128)S(1)} copy-done((s32[32,64,128]{2,1,0:T(8,128)S(1)}, s32[32,64,128]{2,1,0:T(8,128)}, u32[]{:S(2)}) %copy-start.5) | copy-done | bytes 1048600
  51.4 10.2 %fields.1 = (bf16[3,32,64,128]{3,2,1,0:T(8,128)(2,1)}, bf16[3,32,64,128]{3,2,1,0:T(8,128)(2,1)}) custom-call(bf16[3,32,64,128]{3,2,1,0:T(8,128)(2,1)S(1)} %copy-done.1, bf16[3,32,64,128]{3,2,1,0:T(8,128)(2,1)S(1)} %copy-done.3, s32[32,64,128]{2,1,0:T(8,128)S(1)} %copy-done.5, f32[4]{0:T(128)S(1)} %copy-done.9, ...), custom_call_target="tpu_custom_call" | custom-call | tf_op jit(solution)/shard_map/fields/pallas_call | solution.py:349
  61.6 0.0 all-to-all-done
  61.6 1.0 %place.1 = f32[32,512]{1,0:T(8,128)} custom-call(f32[256,128]{1,0:T(8,128)S(1)} %bitcast.3), custom_call_target="tpu_custom_call" | custom-call | tf_op jit(solution)/shard_map/place/pallas_call | solution.py:364
Async XLA Ops:
  0.6 1.4 %copy-start = (bf16[3,32,64,128]{3,2,1,0:T(8,128)(2,1)S(1)}, bf16[3,32,64,128]{3,2,1,0:T(8,128)(2,1)}, u32[]{:S(2)}) copy-start(bf16[3,32,64,128]{3,2,1,0:T(8,128)(2,1)} %e_hbm.3) | copy-start | bytes 4718596
  2.0 1.4 %copy-start.2 = (bf16[3,32,64,128]{3,2,1,0:T(8,128)(2,1)S(1)}, bf16[3,32,64,128]{3,2,1,0:T(8,128)(2,1)}, u32[]{:S(2)}) copy-start(bf16[3,32,64,128]{3,2,1,0:T(8,128)(2,1)} %h_hbm.3) | copy-start | bytes 4718596
  3.5 1.4 %copy-start.4 = (bf16[3,32,64,128]{3,2,1,0:T(8,128)(2,1)S(1)}, bf16[3,32,64,128]{3,2,1,0:T(8,128)(2,1)}, u32[]{:S(2)}) copy-start(bf16[3,32,64,128]{3,2,1,0:T(8,128)(2,1)} %f_hbm.1) | copy-start | bytes 4718596
  4.9 0.9 %copy-start.6 = (s32[8,16,512]{2,1,0:T(8,128)S(1)}, s32[8,16,512]{2,1,0:T(8,128)}, u32[]{:S(2)}) copy-start(s32[8,16,512]{2,1,0:T(8,128)} %tiles_hbm.1) | copy-start | bytes 786436
  5.8 0.9 %copy-start.7 = (s32[65536]{0:T(1024)S(1)}, s32[65536]{0:T(1024)}, u32[]{:S(2)}) copy-start(s32[65536]{0:T(1024)} %param.15) | copy-start | bytes 786436
  6.8 0.7 %copy-start.8 = (s32[32,64]{1,0:T(8,128)S(1)}, s32[32,64]{1,0:T(8,128)}, u32[]{:S(2)}) copy-start(s32[32,64]{1,0:T(8,128)} %slot_ref.1) | copy-start | bytes 24580
  7.5 42.7 %copy-start.1 = (bf16[3,32,64,128]{3,2,1,0:T(8,128)(2,1)S(1)}, bf16[3,32,64,128]{3,2,1,0:T(8,128)(2,1)}, u32[]{:S(2)}) copy-start(bf16[3,32,64,128]{3,2,1,0:T(8,128)(2,1)} %e_hbm.3) | copy-start | bytes 4718596
  7.5 42.7 %copy-start.3 = (bf16[3,32,64,128]{3,2,1,0:T(8,128)(2,1)S(1)}, bf16[3,32,64,128]{3,2,1,0:T(8,128)(2,1)}, u32[]{:S(2)}) copy-start(bf16[3,32,64,128]{3,2,1,0:T(8,128)(2,1)} %h_hbm.3) | copy-start | bytes 4718596
  7.5 42.7 %copy-start.9 = (f32[4]{0:T(128)S(1)}, f32[4]{0:T(128)}, u32[]{:S(2)}) copy-start(f32[4]{0:T(128)} %eps_ref.1) | copy-start | bytes 52
  12.9 0.6 copy-start.10
  13.5 48.1 %all-to-all-start = ((f32[128,2,128]{2,1,0:T(2,128)}), f32[128,2,128]{2,1,0:T(2,128)S(1)}, u32[]{:S(2)}, u32[]{:S(2)}) async-start(f32[128,2,128]{2,1,0:T(2,128)} %bitcast.1), calls=%async_computation | async-start | bytes 262144 | tf_op jit(solution)/shard_map/all_to_all | solution.py:329
  24.1 26.1 %collective-permute-start = (bf16[5,64,128]{2,1,0:T(8,128)(2,1)S(1)}, bf16[5,64,128]{2,1,0:T(8,128)(2,1)S(1)}, u32[]{:S(2)}, u32[]{:S(2)}) collective-permute-start(bf16[5,64,128]{2,1,0:T(8,128)(2,1)S(1)} %get-tuple-element.13), channel_id=1, source_target_pairs={{0,16},{16,0},{32,48},{48,32},{64,80},{80,64},{96,112},{112,96},{1... | collective-permute-start | bytes 245768 | tf_op jit(solution)/shard_map/ppermute | solution.py:335
  24.6 25.5 %collective-permute-start.1 = (bf16[5,64,128]{2,1,0:T(8,128)(2,1)S(1)}, bf16[5,64,128]{2,1,0:T(8,128)(2,1)S(1)}, u32[]{:S(2)}, u32[]{:S(2)}) collective-permute-start(bf16[5,64,128]{2,1,0:T(8,128)(2,1)S(1)} %get-tuple-element.14), channel_id=1, source_target_pairs={{16,32},{32,16},{48,64},{64,48},{80,96},{96,80},{17,33},{33,17},{4... | collective-permute-start | bytes 245768 | tf_op jit(solution)/shard_map/ppermute | solution.py:335
  30.3 19.8 %collective-permute-start.2 = (bf16[5,32,128]{2,1,0:T(8,128)(2,1)}, bf16[5,32,128]{2,1,0:T(8,128)(2,1)S(1)}, u32[]{:S(2)}, u32[]{:S(2)}) collective-permute-start(bf16[5,32,128]{2,1,0:T(8,128)(2,1)} %copy-done.10), channel_id=1, source_target_pairs={{0,1},{1,0},{2,3},{3,2},{4,5},{5,4},{6,7},{7,6},{8,9},{9,8},{10,11... | collective-permute-start | bytes 122888 | tf_op jit(solution)/shard_map/ppermute | solution.py:335
  31.3 18.8 %collective-permute-start.3 = (bf16[5,32,128]{2,1,0:T(8,128)(2,1)S(1)}, bf16[5,32,128]{2,1,0:T(8,128)(2,1)S(1)}, u32[]{:S(2)}, u32[]{:S(2)}) collective-permute-start(bf16[5,32,128]{2,1,0:T(8,128)(2,1)S(1)} %get-tuple-element.16), channel_id=1, source_target_pairs={{1,2},{2,1},{3,4},{4,3},{5,6},{6,5},{7,8},{8,7},{9,10},{10,9},{11,... | collective-permute-start | bytes 122888 | tf_op jit(solution)/shard_map/ppermute | solution.py:335
  33.7 7.9 %collective-permute-start.4 = (f32[8,128]{1,0:T(8,128)S(1)}, f32[8,128]{1,0:T(8,128)S(1)}, u32[]{:S(2)}, u32[]{:S(2)}) collective-permute-start(f32[8,128]{1,0:T(8,128)S(1)} %get-tuple-element.17), channel_id=1, source_target_pairs={{1,16},{16,1},{2,17},{17,2},{3,18},{18,3},{4,19},{19,4},{5,20},{20... | collective-permute-start | bytes 12296 | tf_op jit(solution)/shard_map/ppermute | solution.py:343
  41.6 8.5 %collective-permute-start.5 = (f32[8,128]{1,0:T(8,128)S(1)}, f32[8,128]{1,0:T(8,128)S(1)}, u32[]{:S(2)}, u32[]{:S(2)}) collective-permute-start(f32[8,128]{1,0:T(8,128)S(1)} %get-tuple-element.18), channel_id=1, source_target_pairs={{17,32},{32,17},{18,33},{33,18},{19,34},{34,19},{20,35},{35,20},{2... | collective-permute-start | bytes 12296 | tf_op jit(solution)/shard_map/ppermute | solution.py:343
  50.2 1.2 %copy-start.5 = (s32[32,64,128]{2,1,0:T(8,128)S(1)}, s32[32,64,128]{2,1,0:T(8,128)}, u32[]{:S(2)}) copy-start(s32[32,64,128]{2,1,0:T(8,128)} %m_hbm.1) | copy-start | bytes 3145732

commit v2 on v1

v2 whole, which is shorter than its diff:
```python
import jax
import jax.numpy as jnp
from jax import lax
from jax.experimental import pallas as pl
from jax.experimental.pallas import tpu as pltpu
from jax.sharding import PartitionSpec as P

F32, BF16, I32 = jnp.float32, jnp.bfloat16, jnp.int32
HBM = pl.BlockSpec(memory_space=pltpu.HBM)
VM = pl.BlockSpec(memory_space=pltpu.VMEM)
SM = pl.BlockSpec(memory_space=pltpu.SMEM)
DL = 32
CHUNKS = 8


def split(v):
    hi = v.astype(BF16)
    return hi, (v - hi.astype(F32)).astype(BF16)


def iota(shape, axis):
    return lax.broadcasted_iota(I32, shape, axis)


def dot(a, b):
    return jnp.dot(a, b, preferred_element_type=F32)


def face_kernel(e_hbm, h_hbm, a_ref, b_ref, sem):
    gx = lax.axis_index("gx")
    last = e_hbm.shape[1] - 1

    def fill(up_ref, down_ref):
        copies = [
            pltpu.make_async_copy(e_hbm.at[:, last], up_ref.at[pl.ds(0, 3)], sem.at[0]),
            pltpu.make_async_copy(h_hbm.at[pl.ds(1, 2), last], up_ref.at[pl.ds(3, 2)], sem.at[1]),
            pltpu.make_async_copy(e_hbm.at[pl.ds(1, 2), 0], down_ref.at[pl.ds(0, 2)], sem.at[2]),
        ]
        for one in copies:
            one.start()
        down_ref[pl.ds(2, 3)] = jnp.zeros((3,) + down_ref.shape[1:], BF16)
        for one in copies:
            one.wait()

    @pl.when(gx % 2 == 0)
    def _():
        fill(a_ref, b_ref)

    @pl.when(gx % 2 == 1)
    def _():
        fill(b_ref, a_ref)


def pillar_kernel(
    e_hbm, h_hbm, f_hbm, slot_hbm, tiles_hbm, rank_hbm,
    send_ref, ya_ref, yb_ref, y0_ref,
    e, f, hy, tiles, rank, slot, cells, acc, sem, fsem, msem,
):
    gx, gy = lax.axis_index("gx"), lax.axis_index("gy")
    _, nx, ny, nz = e.shape
    step = nx // CHUNKS
    copies = []
    for i in range(CHUNKS):
        part = pl.ds(i * step, step)
        copies.append((
            pltpu.make_async_copy(e_hbm.at[:, part], e.at[:, part], sem.at[i]),
            pltpu.make_async_copy(f_hbm.at[:, part], f.at[:, part], fsem.at[i]),
        ))
    extra = [
        pltpu.make_async_copy(tiles_hbm.at[gx, pl.ds(gy // 8 * 8, 8)], tiles, msem.at[0]),
        pltpu.make_async_copy(rank_hbm.at[pl.ds(gx * 64, 64)], rank, msem.at[1]),
        pltpu.make_async_copy(slot_hbm, slot, msem.at[2]),
        pltpu.make_async_copy(h_hbm.at[0, :, pl.ds(ny - 8, 8)], hy.at[0], msem.at[3]),
        pltpu.make_async_copy(h_hbm.at[2, :, pl.ds(ny - 8, 8)], hy.at[1], msem.at[4]),
    ]
    for one in extra[:3]:
        one.start()
    for one, two in copies[:1]:
        one.start()
        two.start()
    for one in extra[3:]:
        one.start()
    for one, two in copies[1:]:
        one.start()
        two.start()

    extra[2].wait()
    cells[:, :ny] = slot[...]
    cells[:, ny:] = slot[...]
    half = nx // 2
    lane = iota((half, 2 * ny), 1)
    pair = jnp.where(lane < ny, cells[pl.ds(0, half, stride=2), :], cells[pl.ds(1, half, stride=2), :])

    extra[0].wait()
    extra[1].wait()
    own = jnp.sum(jnp.where(iota(tiles.shape, 0) == gy % 8, tiles[...], 0), axis=0, keepdims=True)
    along_x = own // 512 - gx * 16
    along_y = own % 512 - gy * 32
    quarter = gy // 4
    ranks = jnp.zeros((16, 128), I32)
    for q in range(4):
        ranks = jnp.where(quarter == q, rank[pl.ds(q, 16, stride=4), :], ranks)
    turned = ranks
    for q in range(1, 4):
        turned = jnp.where(gy % 4 == q, pltpu.roll(ranks, 128 - 32 * q, 1), turned)
    square = jnp.concatenate([turned, jnp.zeros((112, 128), I32)], axis=0)
    columns = jnp.transpose(square)[:32]
    slots = own.shape[1]
    found = jnp.zeros((32, slots), I32)
    for q in range(16):
        found = jnp.where(along_x == q, columns[:, q : q + 1], found)
    my_rank = jnp.sum(jnp.where(iota((32, slots), 0) == along_y, found, 0), axis=0, keepdims=True)
    below = jnp.zeros((32, slots), I32)
    for q in range(16):
        below = below + jnp.where(columns[:, q : q + 1] < my_rank, 1, 0)
    order = jnp.sum(below, axis=0, keepdims=True)
    row = jnp.where(own >= 0, (order & 3) * 128 + (order >> 2), -1)
    place = (my_rank & 511).astype(F32)

    acc[...] = jnp.zeros(acc.shape, F32)
    for i, (one, two) in enumerate(copies):
        one.wait()
        two.wait()
        part = pl.ds(i * step, step)
        density = jnp.zeros((step * ny, nz), F32)
        for c in range(3):
            density = density + (
                e[c, part].astype(F32) * f[c, part].astype(F32)
            ).reshape(step * ny, nz)
        hi, lo = split(density)
        both = jnp.concatenate([hi, lo], axis=1)
        hot = jnp.concatenate(
            [
                jnp.where(iota((slots, 128), 0) == pair[p : p + 1], 1.0, 0.0).astype(BF16)
                for p in range(i * step // 2, (i + 1) * step // 2)
            ],
            axis=1,
        )
        acc[...] += dot(hot, both)

    sums = acc[:, :nz] + acc[:, nz:]
    hi, lo = split(sums)
    match = iota((slots, slots), 0) == row
    moved = dot(jnp.where(match, 1.0, 0.0).astype(BF16), jnp.concatenate([hi, lo], axis=1))
    moved = moved[:, :nz] + moved[:, nz:]
    spot = jnp.sum(jnp.where(match, place, 0.0), axis=1, keepdims=True)
    lanes = iota((128, 128), 1)
    values, spots = jnp.zeros((128, 128), F32), jnp.zeros((128, 128), F32)
    for k in range(4):
        hi, lo = split(moved[k * 128 : (k + 1) * 128])
        gather = jnp.where(lanes == 32 * k + iota((128, 128), 0) // 4, 0.125, 0.0).astype(BF16)
        values = values + dot(hi, gather) + dot(lo, gather)
        spots = jnp.where(lanes == k, spot[k * 128 : (k + 1) * 128], spots)
    send_ref[pl.ds(0, 128, stride=2), :] = values
    send_ref[pl.ds(1, 128, stride=2), :] = spots

    for one in extra[3:]:
        one.wait()

    def face(c, y):
        base = y // 8 * 8
        return e[c, :, pl.ds(base, 8), :].astype(F32)[:, y - base, :]

    y0x, y0z = face(0, 0), face(2, 0)
    y0_ref[0] = y0x
    y0_ref[1] = y0z
    last = ny - 1
    up_y = [face(0, last), face(1, last), face(2, last)]
    up_y += [hy[0].astype(F32)[:, 7, :], hy[1].astype(F32)[:, 7, :]]

    def pack(up_ref, down_ref):
        for c in range(5):
            up_ref[pl.ds(c * nx, nx)] = up_y[c].astype(BF16)
        down_ref[pl.ds(0, nx)] = y0x.astype(BF16)
        down_ref[pl.ds(nx, nx)] = y0z.astype(BF16)
        down_ref[pl.ds(2 * nx, 3 * nx)] = jnp.zeros((3 * nx, nz), BF16)
        up_ref[pl.ds(5 * nx, 16)] = jnp.zeros((16, nz), BF16)
        down_ref[pl.ds(5 * nx, 16)] = jnp.zeros((16, nz), BF16)

    @pl.when(gy % 2 == 0)
    def _():
        pack(ya_ref, yb_ref)

    @pl.when(gy % 2 == 1)
    def _():
        pack(yb_ref, ya_ref)


def field_kernel(
    e_hbm, h_hbm, m_hbm, eps_ref, xa_ref, xb_ref, ya_ref, yb_ref, y0_ref,
    ne_hbm, nh_hbm,
    e, h, m, ne, nh, ef, gf, sem, hsem, msem, esem, osem,
):
    gx, gy = lax.axis_index("gx"), lax.axis_index("gy")
    _, nx, ny, nz = h.shape
    step = nx // CHUNKS
    loads, stores = [], []
    for i in range(CHUNKS):
        part = pl.ds(i * step, step)
        loads.append((
            pltpu.make_async_copy(e_hbm.at[:, part], e.at[:, part], sem.at[i]),
            pltpu.make_async_copy(h_hbm.at[:, part], h.at[:, part], hsem.at[i]),
            pltpu.make_async_copy(m_hbm.at[part], m.at[part], msem.at[i]),
        ))
        stores.append((
            pltpu.make_async_copy(nh.at[:, part], nh_hbm.at[:, part], osem.at[i]),
            pltpu.make_async_copy(ne.at[:, part], ne_hbm.at[:, part], esem.at[i]),
        ))
    for group in loads:
        for one in group:
            one.start()

    even_x, even_y = gx % 2 == 0, gy % 2 == 0

    def up_z(v):
        return jnp.where(iota(v.shape, 1) == nz - 1, 0.0, pltpu.roll(v, nz - 1, 1))

    def up_row(v, edge):
        n = v.shape[0]
        return jnp.where(iota(v.shape, 0) == n - 1, edge, pltpu.roll(v, n - 1, 0))

    def either(flag, a, b):
        return jnp.where(flag, a.astype(F32), b.astype(F32))

    def rounded(v):
        return v.astype(BF16).astype(F32)

    ex, ey, ez, hx, hz = [
        either(even_y, yb_ref[pl.ds(c * nx, nx)], ya_ref[pl.ds(c * nx, nx)]) for c in range(5)
    ]
    corner = pl.ds(5 * nx, 16)
    below, above = either(even_y, yb_ref[corner], ya_ref[corner]), either(even_y, ya_ref[corner], yb_ref[corner])
    inside = jnp.where(gy > 0, 1.0, 0.0)
    low_x = rounded(inside * (2.0 * hx - ((y0_ref[1] - ez) - (up_z(ey) - ey))))
    low_z = rounded(inside * (2.0 * hz - ((up_row(ey, below[0:1]) - ey) - (y0_ref[0] - ex))))
    high_x = either(even_y, ya_ref[pl.ds(0, nx)], yb_ref[pl.ds(0, nx)])
    high_z = either(even_y, ya_ref[pl.ds(nx, nx)], yb_ref[pl.ds(nx, nx)])
    for x in range(nx):
        ef[0, x, pl.ds(ny, 1)] = high_x[x : x + 1]
        ef[2, x, pl.ds(ny, 1)] = high_z[x : x + 1]
        gf[0, x + 1, pl.ds(7, 1)] = low_x[x : x + 1]
        gf[2, x + 1, pl.ds(7, 1)] = low_z[x : x + 1]
    rows, kept = pl.ds(0, ny), pl.ds(8, ny)
    for c in range(2):
        ef[c + 1, nx, rows] = either(even_x, xa_ref[c], xb_ref[c])
    ex, ey, ez, hy, hz = [either(even_x, xb_ref[c], xa_ref[c]) for c in range(5)]
    inside = jnp.where(gx > 0, 1.0, 0.0)
    for one in loads[0]:
        one.wait()
    for c in range(3):
        ef[c, 0, rows] = e[c, 0].astype(F32)
    gf[1, 0, kept] = rounded(inside * (2.0 * hy - ((up_z(ex) - ex) - (ef[2, 0, rows] - ez))))
    gf[2, 0, kept] = rounded(inside * (2.0 * hz - ((ef[1, 0, rows] - ey) - (up_row(ex, above[0:1]) - ex))))

    row, col = iota((nz, nz), 0), iota((nz, nz), 1)
    eye = jnp.where(row == col, 1.0, 0.0)
    ahead = jnp.where(row == col + 1, 1.0, 0.0) - eye
    back = eye - jnp.where(row == col - 1, 1.0, 0.0)
    none = jnp.zeros((nz, nz), F32)
    wx = jnp.concatenate([2.0 * eye, ahead], axis=0).astype(BF16)
    wy = jnp.concatenate([2.0 * eye, -ahead], axis=0).astype(BF16)
    wz = jnp.concatenate([2.0 * eye, -eye], axis=0).astype(BF16)
    wb = jnp.concatenate(
        [jnp.concatenate([back, none], axis=1), jnp.concatenate([none, back], axis=1)], axis=0
    ).astype(BF16)
    lane = iota((ny, nz), 1)
    table = jnp.zeros((ny, nz), F32)
    for k in range(4):
        table = jnp.where(lane == k, 0.25 * eps_ref[k], table)

    def first(x):
        if x + 1 < nx:
            for c in range(3):
                ef[c, x + 1, rows] = e[c, x + 1].astype(F32)
        shifted = pl.ds(1, ny)
        fx = dot(jnp.concatenate([h[0, x], e[1, x]], axis=1), wx)
        fy = dot(jnp.concatenate([h[1, x], e[0, x]], axis=1), wy)
        fz = dot(jnp.concatenate([h[2, x], e[0, x]], axis=1), wz)
        ez = ef[2, x, rows]
        fx = fx - (ef[2, x, shifted] - ez)
        fy = fy + (ef[2, x + 1, rows] - ez)
        fz = fz + ef[0, x, shifted] - (ef[1, x + 1, rows] - ef[1, x, rows])
        for c, v in enumerate((fx, fy, fz)):
            g = v.astype(BF16)
            nh[c, x] = g * BF16(0.5)
            gf[c, x + 1, kept] = g.astype(F32)

    def second(x):
        shifted = pl.ds(7, ny)
        pair = jnp.concatenate([nh[0, x], nh[1, x]], axis=1)
        along = dot(pair, wb)
        gx_, gy_, gz_ = [gf[c, x + 1, kept] for c in range(3)]
        coef = jnp.take_along_axis(table, m[x], axis=1)
        tx = (gz_ - gf[2, x + 1, shifted]) - along[:, nz:]
        ty = along[:, :nz] - (gz_ - gf[2, x, kept])
        tz = (gy_ - gf[1, x, kept]) - (gx_ - gf[0, x + 1, shifted])
        for c, t in enumerate((tx, ty, tz)):
            ne[c, x] = (ef[c, x, rows] + coef * t).astype(BF16)

    wb = wb * BF16(2.0)
    for i in range(CHUNKS + 1):
        if i + 1 < CHUNKS:
            for one in loads[i + 1]:
                one.wait()
        for x in range(step):
            if i < CHUNKS:
                first(i * step + x)
            if i > 0:
                second((i - 1) * step + x)
        if i < CHUNKS:
            stores[i][0].start()
        if i > 0:
            stores[i - 1][1].start()
    for group in stores:
        for one in group:
            one.wait()


def place_kernel(got_ref, grad_ref):
    values = jnp.transpose(got_ref[pl.ds(0, 128, stride=2), :])
    spots = got_ref[pl.ds(1, 128, stride=2), :].astype(I32)
    ranks = grad_ref.shape[1]
    total = jnp.zeros((2 * DL, ranks), F32)
    for k in range(4):
        hot = jnp.where(iota((128, ranks), 1) == spots[:, k : k + 1], 1.0, 0.0).astype(BF16)
        hi, lo = split(values[k * DL : (k + 1) * DL])
        total = total + dot(jnp.concatenate([hi, lo], axis=0), hot)
    grad_ref[...] = total[:DL] + total[DL:]


def per_device(
    adjoint_e, adjoint_h, material, inv_eps, forward_design, cell_slot, tile_pillars, pillar_rank
):
    _, nx, ny, nz = adjoint_e.shape
    sx, sy = lax.axis_size("gx"), lax.axis_size("gy")
    both = ("gx", "gy")
    shape = jax.ShapeDtypeStruct

    def stay(v):
        return pltpu.with_memory_space_constraint(v, pltpu.HBM)

    ranks = pillar_rank.reshape(512, 128)
    adjoint_e, adjoint_h, material, forward_design, cell_slot, tile_pillars, ranks = map(
        stay, (adjoint_e, adjoint_h, material, forward_design, cell_slot, tile_pillars, ranks)
    )

    def params(mib):
        return pltpu.CompilerParams(vmem_limit_bytes=mib * 1024 * 1024)

    def swap(v, axis, size, low):
        pairs = []
        for i in range(low, size - 1, 2):
            pairs += [(i, i + 1), (i + 1, i)]
        return lax.ppermute(v, axis, pairs)

    xa, xb = pl.pallas_call(
        face_kernel,
        out_shape=(shape((5, ny, nz), BF16), shape((5, ny, nz), BF16)),
        in_specs=[HBM, HBM],
        out_specs=[VM, VM],
        scratch_shapes=[pltpu.SemaphoreType.DMA((3,))],
        compiler_params=params(4),
        name="faces",
    )(adjoint_e, adjoint_h)
    xa, xb = swap(xa, "gx", sx, 0), swap(xb, "gx", sx, 1)

    send, ya, yb, y0 = pl.pallas_call(
        pillar_kernel,
        out_shape=(
            shape((256, 128), F32),
            shape((5 * nx + 16, nz), BF16), shape((5 * nx + 16, nz), BF16),
            shape((2, nx, nz), F32),
        ),
        in_specs=[HBM] * 6,
        out_specs=[VM] * 4,
        scratch_shapes=[
            pltpu.VMEM((3, nx, ny, nz), BF16), pltpu.VMEM((3, nx, ny, nz), BF16),
            pltpu.VMEM((2, nx, 8, nz), BF16),
            pltpu.VMEM((8, 512), I32), pltpu.VMEM((64, 128), I32), pltpu.VMEM((nx, ny), I32),
            pltpu.VMEM((nx, 2 * ny), I32), pltpu.VMEM((512, 2 * nz), F32),
            pltpu.SemaphoreType.DMA((CHUNKS,)), pltpu.SemaphoreType.DMA((CHUNKS,)),
            pltpu.SemaphoreType.DMA((5,)),
        ],
        compiler_params=params(12),
        name="pillars",
    )(adjoint_e, adjoint_h, forward_design, cell_slot, tile_pillars, ranks)

    got = lax.all_to_all(send.reshape(128, 2, 128), both, 0, 0, tiled=True).reshape(256, 128)

    even_x, even_y = lax.axis_index("gx") % 2 == 0, lax.axis_index("gy") % 2 == 0
    up = jnp.where(even_x, xa[0, ny - 1 :], xb[0, ny - 1 :])
    down = jnp.where(even_x, xb[0, :1], xa[0, :1])
    ya = lax.dynamic_update_slice(ya, jnp.where(even_y, up, down), (5 * nx, 0))
    yb = lax.dynamic_update_slice(yb, jnp.where(even_y, down, up), (5 * nx, 0))
    ya, yb = swap(ya, "gy", sy, 0), swap(yb, "gy", sy, 1)

    new_e, new_h = pl.pallas_call(
        field_kernel,
        out_shape=(shape(adjoint_e.shape, BF16), shape(adjoint_e.shape, BF16)),
        in_specs=[HBM, HBM, HBM, SM] + [VM] * 5,
        out_specs=[HBM, HBM],
        scratch_shapes=[
            pltpu.VMEM((3, nx, ny, nz), BF16), pltpu.VMEM((3, nx, ny, nz), BF16),
            pltpu.VMEM((nx, ny, nz), I32),
            pltpu.VMEM((3, nx, ny, nz), BF16), pltpu.VMEM((3, nx, ny, nz), BF16),
            pltpu.VMEM((3, nx + 1, ny + 8, nz), F32), pltpu.VMEM((3, nx + 1, ny + 8, nz), F32),
        ] + [pltpu.SemaphoreType.DMA((CHUNKS,))] * 5,
        compiler_params=params(20),
        name="fields",
    )(adjoint_e, adjoint_h, material, inv_eps, xa, xb, ya, yb, y0)

    gradient = pl.pallas_call(
        place_kernel,
        out_shape=shape((DL, 512), F32),
        in_specs=[VM],
        out_specs=VM,
        compiler_params=params(4),
        name="place",
    )(got)
    return new_e, new_h, gradient


def solution(mesh):
    return jax.shard_map(
        per_device,
        mesh=mesh,
        in_specs=(
            P(None, "gx", "gy", None),
            P(None, "gx", "gy", None),
            P("gx", "gy", None),
            P(),
            P(None, "gx", "gy", None),
            P("gx", "gy"),
            P(),
            P(),
        ),
        out_specs=(P(None, "gx", "gy", None), P(None, "gx", "gy", None), P(None, ("gx", "gy"))),
        check_vma=False,
    )
```

time: 63 us -> 36.2 us (0.57)
  the two profiles are of different devices: /device:TPU:31 before, /device:TPU:7 now
where the time goes in v2:
time: 36.2 us; the launch traced here: 36 us
  starting transfers between devices  18.2 us (50%)
  Pallas kernels  12.8 us (35%)
  waiting for transfers between devices  4.16 us (11%)
  between operations  0.75 us (2%)
    all_to_all x1, starting transfers between devices, per_device(): lax.all_to_all(send.reshape(128, 2, 128), both, 0, 0, tiled=True)  12.6 us
    pallas_call x1, Pallas kernels, per_device(): pl.pallas_call(field_kernel, out_shape=(shape(adjoint_e.shape, BF16), sha...  5.63 us
    ppermute x4, starting transfers between devices, swap(): return lax.ppermute(v, axis, pairs)  5.59 us
    pallas_call x1, Pallas kernels, per_device(): pl.pallas_call(pillar_kernel, out_shape=(shape((256, 128), F32), shape((5...  5.34 us
    ppermute x4, waiting for transfers between devices, swap(): return lax.ppermute(v, axis, pairs)  4.16 us
    pallas_call x1, Pallas kernels, per_device(): pl.pallas_call(place_kernel, out_shape=shape((DL, 512), F32), in_specs=[V...  0.97 us
    pallas_call x1, Pallas kernels, per_device(): pl.pallas_call(face_kernel, out_shape=(shape((5, ny, nz), BF16), shape((5...  0.85 us
  transfers between devices with their start and end apart: 5, of which 1 were waited for; matrix products, arithmetic and copies ran while one was open for 0% of the time, Pallas kernels for 30%

profile of v2, /device:TPU:7, one launch (start us, length us, event | category | flops | bytes accessed | tf_op | source)
XLA Modules:
  0.0 36.0 jit_solution(13192565409490620148)
XLA Ops:
  0.6 0.8 %faces.1 = (bf16[5,64,128]{2,1,0:T(8,128)(2,1)S(1)}, bf16[5,64,128]{2,1,0:T(8,128)(2,1)S(1)}) custom-call(bf16[3,32,64,128]{3,2,1,0:T(8,128)(2,1)} %e_hbm.5, bf16[3,32,64,128]{3,2,1,0:T(8,128)(2,1)} %h_hbm.5), custom_call_target="tpu_custom_call" | custom-call | tf_op jit(solution)/shard_map/faces/pallas_call | solution.py:356
  1.5 1.4 %collective-permute-start = (bf16[5,64,128]{2,1,0:T(8,128)(2,1)S(1)}, bf16[5,64,128]{2,1,0:T(8,128)(2,1)S(1)}, u32[]{:S(2)}, u32[]{:S(2)}) collective-permute-start(bf16[5,64,128]{2,1,0:T(8,128)(2,1)S(1)} %get-tuple-element.11), channel_id=1, source_target_pairs={{0,16},{16,0},{32,48},{48,32},{64,80},{80,64},{96,112},{112,96},{1... | collective-permute-start | bytes 245768 | tf_op jit(solution)/shard_map/ppermute | solution.py:354
  2.9 0.7 %collective-permute-start.1 = (bf16[5,64,128]{2,1,0:T(8,128)(2,1)S(1)}, bf16[5,64,128]{2,1,0:T(8,128)(2,1)S(1)}, u32[]{:S(2)}, u32[]{:S(2)}) collective-permute-start(bf16[5,64,128]{2,1,0:T(8,128)(2,1)S(1)} %get-tuple-element.12), channel_id=1, source_target_pairs={{16,32},{32,16},{48,64},{64,48},{80,96},{96,80},{17,33},{33,17},{4... | collective-permute-start | bytes 245768 | tf_op jit(solution)/shard_map/ppermute | solution.py:354
  3.5 0.0 copy-start
  3.5 5.3 %pillars.1 = (f32[256,128]{1,0:T(8,128)}, bf16[176,128]{1,0:T(8,128)(2,1)S(1)}, bf16[176,128]{1,0:T(8,128)(2,1)S(1)}, f32[2,32,128]{2,1,0:T(8,128)S(1)}) custom-call(bf16[3,32,64,128]{3,2,1,0:T(8,128)(2,1)} %e_hbm.5, bf16[3,32,64,128]{3,2,1,0:T(8,128)(2,1)} %h_hbm.5, bf16[3,32,64,128]{3,2,1,0:T(8,128)(2,1)} %f_hbm.1, s32[32,64]{1,0:T(8,128)} %slot_hbm.1, ...), custom_call_target="tpu_custom_call" | custom-call | tf_op jit(solution)/shard_map/pillars/pallas_call | solution.py:367
  8.9 12.6 %all-to-all-start = ((f32[128,2,128]{2,1,0:T(2,128)}), f32[128,2,128]{2,1,0:T(2,128)S(1)}, u32[]{:S(2)}, u32[]{:S(2)}) async-start(f32[128,2,128]{2,1,0:T(2,128)} %bitcast.3), calls=%async_computation | async-start | bytes 262144 | tf_op jit(solution)/shard_map/all_to_all | solution.py:388
  21.5 0.0 collective-permute-done.xa_ref
  21.5 0.0 collective-permute-done.1.xb_ref
  21.6 3.5 %collective-permute-start.3 = (bf16[176,128]{1,0:T(8,128)(2,1)S(1)}, bf16[176,128]{1,0:T(8,128)(2,1)S(1)}, u32[]{:S(2)}, u32[]{:S(2)}) collective-permute-start(bf16[176,128]{1,0:T(8,128)(2,1)S(1)} %dynamic_update_slice.7), channel_id=1, source_target_pairs={{1,2},{2,1},{3,4},{4,3},{5,6},{6,5},{7,8},{8,7},{9,10},{10,9},{11,... | collective-permute-start | bytes 135176 | tf_op jit(solution)/shard_map/ppermute | solution.py:354
  25.1 0.1 collective-permute-start.2
  25.2 4.2 %collective-permute-done.3.yb_ref = bf16[176,128]{1,0:T(8,128)(2,1)S(1)} collective-permute-done((bf16[176,128]{1,0:T(8,128)(2,1)S(1)}, bf16[176,128]{1,0:T(8,128)(2,1)S(1)}, u32[]{:S(2)}, u32[]{:S(2)}) %collective-permute-start.3) | collective-permute-done | bytes 45088 | tf_op jit(solution)/shard_map/ppermute | solution.py:354
  29.4 0.0 collective-permute-done.2.ya_ref
  29.4 0.0 copy-done
  29.4 5.6 %fields.1 = (bf16[3,32,64,128]{3,2,1,0:T(8,128)(2,1)}, bf16[3,32,64,128]{3,2,1,0:T(8,128)(2,1)}) custom-call(bf16[3,32,64,128]{3,2,1,0:T(8,128)(2,1)} %e_hbm.5, bf16[3,32,64,128]{3,2,1,0:T(8,128)(2,1)} %h_hbm.5, s32[32,64,128]{2,1,0:T(8,128)} %m_hbm.1, f32[4]{0:T(128)S(1)} %copy-done, bf16[5,64,128]{2,1,0:T(8,128)(2,1)S(1)} %collective-permute-done.xa_ref, ...), custom_call_target="tpu_custom_call" | custom-call | tf_op jit(solution)/shard_map/fields/pallas_call | solution.py:397
  35.0 0.0 all-to-all-done
  35.0 1.0 %place.1 = f32[32,512]{1,0:T(8,128)} custom-call(f32[256,128]{1,0:T(8,128)S(1)} %bitcast.7), custom_call_target="tpu_custom_call" | custom-call | tf_op jit(solution)/shard_map/place/pallas_call | solution.py:412
  (3 shorter events, 0.1 us)
Async XLA Ops:
  1.5 20.1 %collective-permute-start = (bf16[5,64,128]{2,1,0:T(8,128)(2,1)S(1)}, bf16[5,64,128]{2,1,0:T(8,128)(2,1)S(1)}, u32[]{:S(2)}, u32[]{:S(2)}) collective-permute-start(bf16[5,64,128]{2,1,0:T(8,128)(2,1)S(1)} %get-tuple-element.11), channel_id=1, source_target_pairs={{0,16},{16,0},{32,48},{48,32},{64,80},{80,64},{96,112},{112,96},{1... | collective-permute-start | bytes 245768 | tf_op jit(solution)/shard_map/ppermute | solution.py:354
  2.9 18.7 %collective-permute-start.1 = (bf16[5,64,128]{2,1,0:T(8,128)(2,1)S(1)}, bf16[5,64,128]{2,1,0:T(8,128)(2,1)S(1)}, u32[]{:S(2)}, u32[]{:S(2)}) collective-permute-start(bf16[5,64,128]{2,1,0:T(8,128)(2,1)S(1)} %get-tuple-element.12), channel_id=1, source_target_pairs={{16,32},{32,16},{48,64},{64,48},{80,96},{96,80},{17,33},{33,17},{4... | collective-permute-start | bytes 245768 | tf_op jit(solution)/shard_map/ppermute | solution.py:354
  3.5 25.8 %copy-start = (f32[4]{0:T(128)S(1)}, f32[4]{0:T(128)}, u32[]{:S(2)}) copy-start(f32[4]{0:T(128)} %eps_ref.1) | copy-start | bytes 52
  8.9 26.1 %all-to-all-start = ((f32[128,2,128]{2,1,0:T(2,128)}), f32[128,2,128]{2,1,0:T(2,128)S(1)}, u32[]{:S(2)}, u32[]{:S(2)}) async-start(f32[128,2,128]{2,1,0:T(2,128)} %bitcast.3), calls=%async_computation | async-start | bytes 262144 | tf_op jit(solution)/shard_map/all_to_all | solution.py:388
  21.6 7.8 %collective-permute-start.3 = (bf16[176,128]{1,0:T(8,128)(2,1)S(1)}, bf16[176,128]{1,0:T(8,128)(2,1)S(1)}, u32[]{:S(2)}, u32[]{:S(2)}) collective-permute-start(bf16[176,128]{1,0:T(8,128)(2,1)S(1)} %dynamic_update_slice.7), channel_id=1, source_target_pairs={{1,2},{2,1},{3,4},{4,3},{5,6},{6,5},{7,8},{8,7},{9,10},{10,9},{11,... | collective-permute-start | bytes 135176 | tf_op jit(solution)/shard_map/ppermute | solution.py:354
  25.1 4.2 %collective-permute-start.2 = (bf16[176,128]{1,0:T(8,128)(2,1)S(1)}, bf16[176,128]{1,0:T(8,128)(2,1)S(1)}, u32[]{:S(2)}, u32[]{:S(2)}) collective-permute-start(bf16[176,128]{1,0:T(8,128)(2,1)S(1)} %dynamic_update_slice.6), channel_id=1, source_target_pairs={{0,1},{1,0},{2,3},{3,2},{4,5},{5,4},{6,7},{7,6},{8,9},{9,8},{10,11... | collective-permute-start | bytes 135176 | tf_op jit(solution)/shard_map/ppermute | solution.py:354

commit v3 on v2

v3 whole, which is shorter than its diff:
```python
import jax
import jax.numpy as jnp
from jax import lax
from jax.experimental import pallas as pl
from jax.experimental.pallas import tpu as pltpu
from jax.sharding import PartitionSpec as P

F32, BF16, I32 = jnp.float32, jnp.bfloat16, jnp.int32
HBM = pl.BlockSpec(memory_space=pltpu.HBM)
VM = pl.BlockSpec(memory_space=pltpu.VMEM)
SM = pl.BlockSpec(memory_space=pltpu.SMEM)
DL = 32
CHUNKS = 8
PARTS = 4


def split(v):
    hi = v.astype(BF16)
    return hi, (v - hi.astype(F32)).astype(BF16)


def iota(shape, axis):
    return lax.broadcasted_iota(I32, shape, axis)


def dot(a, b):
    return jnp.dot(a, b, preferred_element_type=F32)


def face_kernel(e_hbm, h_hbm, a_ref, b_ref, sem):
    gx = lax.axis_index("gx")
    last = e_hbm.shape[1] - 1

    def fill(up_ref, down_ref):
        copies = [
            pltpu.make_async_copy(e_hbm.at[:, last], up_ref.at[pl.ds(0, 3)], sem.at[0]),
            pltpu.make_async_copy(h_hbm.at[pl.ds(1, 2), last], up_ref.at[pl.ds(3, 2)], sem.at[1]),
            pltpu.make_async_copy(e_hbm.at[pl.ds(1, 2), 0], down_ref.at[pl.ds(0, 2)], sem.at[2]),
        ]
        for one in copies:
            one.start()
        down_ref[pl.ds(2, 3)] = jnp.zeros((3,) + down_ref.shape[1:], BF16)
        for one in copies:
            one.wait()

    @pl.when(gx % 2 == 0)
    def _():
        fill(a_ref, b_ref)

    @pl.when(gx % 2 == 1)
    def _():
        fill(b_ref, a_ref)


def lookup(table, index):
    rows = index.shape[0]
    result = jnp.zeros(index.shape, table.dtype)
    for q in range(4):
        part = jnp.broadcast_to(table[q : q + 1], (rows, 128))
        taken = jnp.take_along_axis(part, index & 127, axis=1, mode="promise_in_bounds")
        result = jnp.where(index >> 7 == q, taken, result)
    return result


def pillar_kernel(
    e_hbm, h_hbm, f_hbm, slot_hbm, tiles_hbm, rank_hbm,
    send_ref, ya_ref, yb_ref, y0_ref,
    e, f, y_first, y_last, y_h, tiles, rank, slot, cells, ids, acc, sem, fsem, msem,
):
    gx, gy = lax.axis_index("gx"), lax.axis_index("gy")
    _, nx, ny, nz = e.shape
    parts = sem.shape[0]
    step = nx // parts
    copies = []
    for i in range(parts):
        part = pl.ds(i * step, step)
        copies.append((
            pltpu.make_async_copy(e_hbm.at[:, part], e.at[:, part], sem.at[i]),
            pltpu.make_async_copy(f_hbm.at[:, part], f.at[:, part], fsem.at[i]),
        ))
    extra = [
        pltpu.make_async_copy(tiles_hbm.at[gx, pl.ds(gy // 8 * 8, 8)], tiles, msem.at[0]),
        pltpu.make_async_copy(rank_hbm.at[pl.ds(gx * 64, 64)], rank, msem.at[1]),
        pltpu.make_async_copy(slot_hbm, slot, msem.at[2]),
        pltpu.make_async_copy(e_hbm.at[:, :, pl.ds(0, 8)], y_first, msem.at[3]),
        pltpu.make_async_copy(e_hbm.at[:, :, pl.ds(ny - 8, 8)], y_last, msem.at[4]),
        pltpu.make_async_copy(h_hbm.at[0, :, pl.ds(ny - 8, 8)], y_h.at[0], msem.at[5]),
        pltpu.make_async_copy(h_hbm.at[2, :, pl.ds(ny - 8, 8)], y_h.at[1], msem.at[6]),
    ]
    for one in extra[:3]:
        one.start()
    for one, two in copies[:1]:
        one.start()
        two.start()
    for one in extra[3:]:
        one.start()
    for one, two in copies[1:]:
        one.start()
        two.start()
    ids[...] = iota(ids.shape, 0)
    lanes, rows = iota((128, 128), 1), iota((128, 128), 0)

    for one in extra[:3]:
        one.wait()
    quarter = gy // 4
    ranks = rank[pl.ds(0, 16, stride=4), :]
    for q in range(1, 4):
        ranks = jnp.where(quarter == q, rank[pl.ds(q, 16, stride=4), :], ranks)
    turned = ranks
    for q in range(1, 4):
        turned = jnp.where(gy % 4 == q, pltpu.roll(ranks, 128 - 32 * q, 1), turned)
    moved = [turned] + [pltpu.roll(turned, 32 * q, 1) for q in range(1, 4)]
    lane = iota((1, 128), 1)
    own_rank = []
    for q in range(4):
        line = moved[0][4 * q : 4 * q + 1]
        for k in range(1, 4):
            line = jnp.where(lane >> 5 == k, moved[k][4 * q + k : 4 * q + k + 1], line)
        own_rank.append(line)
    owner = [line >> 9 for line in own_rank]
    hits = [rows == line for line in owner]
    ones = [jnp.where(hit, 1.0, 0.0).astype(BF16) for hit in hits]
    counter = jnp.concatenate(
        [jnp.where(rows < lanes, 1.0, 0.0), jnp.ones((128, 128), F32)], axis=1
    ).astype(BF16)
    before = jnp.zeros((128, 128), F32)
    turn = []
    for q in range(4):
        both = dot(ones[q], counter)
        count = both[:, :128] + before
        turn.append(jnp.sum(jnp.where(hits[q], count, 0.0), axis=0, keepdims=True).astype(I32))
        before = before + both[:, 128:]
    spots = []
    for q in range(4):
        place = own_rank[q] & 511
        eight = jnp.where(iota((16, 128), 0) < 4, place & 255, place & 256)
        mine = (iota((16, 128), 0) & 3 == turn[q]) & (iota((16, 128), 0) < 8)
        spots.append(jnp.where(mine, eight, 0).astype(F32).astype(BF16))
    spots = lax.dot_general(
        jnp.concatenate(ones, axis=1), jnp.concatenate(spots, axis=1),
        (((1,), (1,)), ((), ())), preferred_element_type=F32,
    )
    send_ref[pl.ds(1, 128, stride=2), :] = jnp.concatenate([spots, jnp.zeros((128, 112), F32)], axis=1)
    target = jnp.concatenate([turn[q] * 128 + owner[q] for q in range(4)], axis=0)
    own = jnp.sum(jnp.where(iota(tiles.shape, 0) == gy % 8, tiles[...], 0), axis=0, keepdims=True)
    own = jnp.concatenate([own[:, 128 * q : 128 * (q + 1)] for q in range(4)], axis=0)
    canon = ((own >> 9) & 15) * 32 + (own & 31)
    target = lookup(target, canon)
    cells[:, :ny] = slot[...]
    cells[:, ny:] = slot[...]
    half = nx // 2
    pair = jnp.where(
        iota((half, 2 * ny), 1) < ny,
        cells[pl.ds(0, half, stride=2), :], cells[pl.ds(1, half, stride=2), :],
    )
    pair = lookup(target, pair)

    for i, (one, two) in enumerate(copies):
        one.wait()
        two.wait()
        part = pl.ds(i * step, step)
        density = e[0, part].astype(F32) * f[0, part].astype(F32)
        for c in range(1, 3):
            density = density + e[c, part].astype(F32) * f[c, part].astype(F32)
        both = jnp.concatenate(split(density.reshape(step * ny, nz)), axis=1)
        hot = jnp.concatenate(
            [
                jnp.where(ids[...] == pair[p : p + 1], 1.0, 0.0).astype(BF16)
                for p in range(i * step // 2, (i + 1) * step // 2)
            ],
            axis=1,
        )
        total = dot(hot, both)
        if i == 0:
            acc[...] = total
        elif i + 1 < parts:
            acc[...] += total
    total = acc[...] + total
    values = jnp.zeros((128, 128), F32)
    for k in range(4):
        part = total[k * 128 : (k + 1) * 128]
        hi, lo = split(part[:, :nz] + part[:, nz:])
        gather = jnp.where(lanes == 32 * k + (rows >> 2), 0.125, 0.0).astype(BF16)
        values = values + dot(hi, gather) + dot(lo, gather)
    send_ref[pl.ds(0, 128, stride=2), :] = values

    for one in extra[3:]:
        one.wait()
    at = iota((nx, 8 * nx), 1) - 8 * iota((nx, 8 * nx), 0)
    low = jnp.where(at == 0, 1.0, 0.0).astype(BF16)
    high = jnp.where(at == 7, 1.0, 0.0).astype(BF16)

    def face(which, one, two):
        both = jnp.concatenate([one.reshape(8 * nx, nz), two.reshape(8 * nx, nz)], axis=1)
        both = dot(which, both)
        return both[:, :nz], both[:, nz:]

    y0x, y0z = face(low, y_first[0], y_first[2])
    up_y = face(high, y_last[0], y_last[1]) + face(high, y_last[2], y_h[0]) + face(high, y_h[1], y_h[1])[:1]
    y0_ref[0] = y0x
    y0_ref[1] = y0z

    def pack(up_ref, down_ref):
        for c in range(5):
            up_ref[pl.ds(c * nx, nx)] = up_y[c].astype(BF16)
        down_ref[pl.ds(0, nx)] = y0x.astype(BF16)
        down_ref[pl.ds(nx, nx)] = y0z.astype(BF16)
        down_ref[pl.ds(2 * nx, 3 * nx)] = jnp.zeros((3 * nx, nz), BF16)
        up_ref[pl.ds(5 * nx, 16)] = jnp.zeros((16, nz), BF16)
        down_ref[pl.ds(5 * nx, 16)] = jnp.zeros((16, nz), BF16)

    @pl.when(gy % 2 == 0)
    def _():
        pack(ya_ref, yb_ref)

    @pl.when(gy % 2 == 1)
    def _():
        pack(yb_ref, ya_ref)


def eye_like(distance, n):
    return jnp.where(iota((n, n), 0) == iota((n, n), 1) + distance, 1.0, 0.0)


def square(a, b, c, d):
    top, bottom = jnp.concatenate([a, b], axis=1), jnp.concatenate([c, d], axis=1)
    return jnp.concatenate([top, bottom], axis=0).astype(BF16)


def side(one, two):
    shape = (one.shape[0] * one.shape[1], one.shape[2])
    return jnp.concatenate([one.reshape(shape), two.reshape(shape)], axis=1)


def spread_kernel(e_hbm, h_hbm, ef_ref, hf_ref, e, h, sem, hsem):
    _, nx, ny, nz = h.shape
    parts = sem.shape[0]
    step = nx // parts
    loads = []
    for i in range(parts):
        part = pl.ds(i * step, step)
        loads.append((
            pltpu.make_async_copy(e_hbm.at[:, part], e.at[:, part], sem.at[i]),
            pltpu.make_async_copy(h_hbm.at[:, part], h.at[:, part], hsem.at[i]),
        ))
    for group in loads:
        for one in group:
            one.start()
    eye = eye_like(0, nz)
    ahead = eye_like(1, nz) - eye
    none = jnp.zeros((nz, nz), F32)
    wx = square(2.0 * eye, none, ahead, eye)
    wy = square(2.0 * eye, none, -ahead, eye)
    for i in range(parts):
        for one in loads[i]:
            one.wait()
        part = pl.ds(i * step, step)
        for c, other, w in ((0, 1, wx), (1, 0, wy)):
            both = dot(side(h[c, part], e[other, part]), w)
            for k in range(step):
                x = i * step + k
                line = both[k * ny : (k + 1) * ny]
                hf_ref[c, x] = line[:, :nz]
                ef_ref[other, x, pl.ds(0, ny)] = line[:, nz:]
        for k in range(step):
            x = i * step + k
            hz = h[2, x].astype(F32)
            hf_ref[2, x] = hz + hz
            ef_ref[2, x, pl.ds(0, ny)] = e[2, x].astype(F32)


def field_kernel(
    ef, hf, m_hbm, eps_ref, xa_ref, xb_ref, ya_ref, yb_ref, y0_ref,
    ne_hbm, nh_hbm,
    m, ne, nh, gf, high, beyond, msem, esem, osem,
):
    gx, gy = lax.axis_index("gx"), lax.axis_index("gy")
    nx, ny, nz = m.shape
    parts = msem.shape[0]
    step = nx // parts
    loads, stores = [], []
    for i in range(parts):
        part = pl.ds(i * step, step)
        loads.append(pltpu.make_async_copy(m_hbm.at[part], m.at[part], msem.at[i]))
        stores.append((
            pltpu.make_async_copy(nh.at[:, part], nh_hbm.at[:, part], osem.at[i]),
            pltpu.make_async_copy(ne.at[:, part], ne_hbm.at[:, part], esem.at[i]),
        ))
    for one in loads:
        one.start()

    even_x, even_y = gx % 2 == 0, gy % 2 == 0
    rows, kept = pl.ds(0, ny), pl.ds(8, ny)

    def up_z(v):
        return jnp.where(iota(v.shape, 1) == nz - 1, 0.0, pltpu.roll(v, nz - 1, 1))

    def up_row(v, edge):
        n = v.shape[0]
        return jnp.where(iota(v.shape, 0) == n - 1, edge, pltpu.roll(v, n - 1, 0))

    def either(flag, a, b):
        return jnp.where(flag, a.astype(F32), b.astype(F32))

    def rounded(v):
        return v.astype(BF16).astype(F32)

    ex, ey, ez, hx, hz = [
        either(even_y, yb_ref[pl.ds(c * nx, nx)], ya_ref[pl.ds(c * nx, nx)]) for c in range(5)
    ]
    corner = pl.ds(5 * nx, 16)
    below, above = either(even_y, yb_ref[corner], ya_ref[corner]), either(even_y, ya_ref[corner], yb_ref[corner])
    inside = jnp.where(gy > 0, 1.0, 0.0)
    low_x = rounded(inside * (2.0 * hx - ((y0_ref[1] - ez) - (up_z(ey) - ey))))
    low_z = rounded(inside * (2.0 * hz - ((up_row(ey, below[0:1]) - ey) - (y0_ref[0] - ex))))
    high[0] = either(even_y, ya_ref[pl.ds(0, nx)], yb_ref[pl.ds(0, nx)])
    high[1] = either(even_y, ya_ref[pl.ds(nx, nx)], yb_ref[pl.ds(nx, nx)])
    for x in range(nx):
        gf[0, x + 1, pl.ds(7, 1)] = low_x[x : x + 1]
        gf[2, x + 1, pl.ds(7, 1)] = low_z[x : x + 1]
    for c in range(2):
        beyond[c] = either(even_x, xa_ref[c], xb_ref[c])
    ex, ey, ez, hy, hz = [either(even_x, xb_ref[c], xa_ref[c]) for c in range(5)]
    inside = jnp.where(gx > 0, 1.0, 0.0)
    gf[1, 0, kept] = rounded(inside * (2.0 * hy - ((up_z(ex) - ex) - (ef[2, 0, rows] - ez))))
    gf[2, 0, kept] = rounded(inside * (2.0 * hz - ((ef[1, 0, rows] - ey) - (up_row(ex, above[0:1]) - ex))))

    back = 2.0 * (eye_like(0, nz) - eye_like(-1, nz))
    none = jnp.zeros((nz, nz), F32)
    wb = square(back, none, none, back)
    lane = iota((ny, nz), 1)
    table = jnp.zeros((ny, nz), F32)
    for k in range(4):
        table = jnp.where(lane == k, 0.25 * eps_ref[k], table)
    seventh = iota((8, nz), 0) == 7

    def up_y(c, which, x):
        last = jnp.where(seventh, high[which, pl.ds(x, 1)], ef[c, x, pl.ds(ny - 7, 8)])
        return jnp.concatenate([ef[c, x, pl.ds(1, ny - 8)], last], axis=0)

    def first(x):
        ey, ez = ef[1, x, rows], ef[2, x, rows]
        eyn = ef[1, x + 1, rows] if x + 1 < nx else beyond[0]
        ezn = ef[2, x + 1, rows] if x + 1 < nx else beyond[1]
        fx = hf[0, x] - (up_y(2, 1, x) - ez)
        fy = hf[1, x] + (ezn - ez)
        fz = (hf[2, x] + (up_y(0, 0, x) - ef[0, x, rows])) - (eyn - ey)
        for c, v in enumerate((fx, fy, fz)):
            g = v.astype(BF16)
            nh[c, x] = g * BF16(0.5)
            gf[c, x + 1, kept] = g.astype(F32)

    picks = lax.GatherDimensionNumbers(
        offset_dims=(), collapsed_slice_dims=(1,), start_index_map=(1,),
        operand_batching_dims=(0,), start_indices_batching_dims=(0,),
    )

    def second(x, along):
        shifted = pl.ds(7, ny)
        gx_, gy_, gz_ = [gf[c, x + 1, kept] for c in range(3)]
        coef = lax.gather(
            table, m[x][..., None], picks, (1, 1), mode=lax.GatherScatterMode.PROMISE_IN_BOUNDS
        )
        tx = (gz_ - gf[2, x + 1, shifted]) - along[:, nz:]
        ty = along[:, :nz] - (gz_ - gf[2, x, kept])
        tz = (gy_ - gf[1, x, kept]) - (gx_ - gf[0, x + 1, shifted])
        for c, t in enumerate((tx, ty, tz)):
            ne[c, x] = (ef[c, x, rows] + coef * t).astype(BF16)

    for i in range(parts + 1):
        if i > 0:
            loads[i - 1].wait()
            part = pl.ds((i - 1) * step, step)
            along = dot(side(nh[0, part], nh[1, part]), wb)
        for k in range(step):
            if i < parts:
                first(i * step + k)
            if i > 0:
                second((i - 1) * step + k, along[k * ny : (k + 1) * ny])
        if i < parts:
            stores[i][0].start()
        if i > 0:
            stores[i - 1][1].start()
    for group in stores:
        for one in group:
            one.wait()


def place_kernel(got_ref, grad_ref):
    values = jnp.transpose(got_ref[pl.ds(0, 128, stride=2), :])
    spots = got_ref[pl.ds(1, 128, stride=2), :].astype(I32)
    spots = spots[:, :4] + spots[:, 4:8]
    ranks = grad_ref.shape[1]
    total = jnp.zeros((2 * DL, ranks), F32)
    for k in range(4):
        hot = jnp.where(iota((128, ranks), 1) == spots[:, k : k + 1], 1.0, 0.0).astype(BF16)
        hi, lo = split(values[k * DL : (k + 1) * DL])
        total = total + dot(jnp.concatenate([hi, lo], axis=0), hot)
    grad_ref[...] = total[:DL] + total[DL:]


def per_device(
    adjoint_e, adjoint_h, material, inv_eps, forward_design, cell_slot, tile_pillars, pillar_rank
):
    _, nx, ny, nz = adjoint_e.shape
    sx, sy = lax.axis_size("gx"), lax.axis_size("gy")
    both = ("gx", "gy")
    shape = jax.ShapeDtypeStruct

    def stay(v):
        return pltpu.with_memory_space_constraint(v, pltpu.HBM)

    ranks = pillar_rank.reshape(512, 128)
    adjoint_e, adjoint_h, material, forward_design, cell_slot, tile_pillars, ranks = map(
        stay, (adjoint_e, adjoint_h, material, forward_design, cell_slot, tile_pillars, ranks)
    )

    def params(mib):
        return pltpu.CompilerParams(vmem_limit_bytes=mib * 1024 * 1024)

    def swap(v, axis, size, low):
        pairs = []
        for i in range(low, size - 1, 2):
            pairs += [(i, i + 1), (i + 1, i)]
        return lax.ppermute(v, axis, pairs)

    xa, xb = pl.pallas_call(
        face_kernel,
        out_shape=(shape((5, ny, nz), BF16), shape((5, ny, nz), BF16)),
        in_specs=[HBM, HBM],
        out_specs=[VM, VM],
        scratch_shapes=[pltpu.SemaphoreType.DMA((3,))],
        compiler_params=params(4),
        name="faces",
    )(adjoint_e, adjoint_h)
    xa, xb = swap(xa, "gx", sx, 0), swap(xb, "gx", sx, 1)

    send, ya, yb, y0 = pl.pallas_call(
        pillar_kernel,
        out_shape=(
            shape((256, 128), F32),
            shape((5 * nx + 16, nz), BF16), shape((5 * nx + 16, nz), BF16),
            shape((2, nx, nz), F32),
        ),
        in_specs=[HBM] * 6,
        out_specs=[VM] * 4,
        scratch_shapes=[
            pltpu.VMEM((3, nx, ny, nz), BF16), pltpu.VMEM((3, nx, ny, nz), BF16),
            pltpu.VMEM((3, nx, 8, nz), BF16), pltpu.VMEM((3, nx, 8, nz), BF16),
            pltpu.VMEM((2, nx, 8, nz), BF16),
            pltpu.VMEM((8, 512), I32), pltpu.VMEM((64, 128), I32), pltpu.VMEM((nx, ny), I32),
            pltpu.VMEM((nx, 2 * ny), I32), pltpu.VMEM((512, 128), I32),
            pltpu.VMEM((512, 2 * nz), F32),
            pltpu.SemaphoreType.DMA((PARTS,)), pltpu.SemaphoreType.DMA((PARTS,)),
            pltpu.SemaphoreType.DMA((7,)),
        ],
        compiler_params=params(12),
        name="pillars",
    )(adjoint_e, adjoint_h, forward_design, cell_slot, tile_pillars, ranks)

    got = lax.all_to_all(send.reshape(128, 2, 128), both, 0, 0, tiled=True)
    got = got.reshape(256, 128)

    even_x, even_y = lax.axis_index("gx") % 2 == 0, lax.axis_index("gy") % 2 == 0
    up = jnp.where(even_x, xa[0, ny - 1 :], xb[0, ny - 1 :])
    down = jnp.where(even_x, xb[0, :1], xa[0, :1])
    ya = lax.dynamic_update_slice(ya, jnp.where(even_y, up, down), (5 * nx, 0))
    yb = lax.dynamic_update_slice(yb, jnp.where(even_y, down, up), (5 * nx, 0))
    ya = swap(ya, "gy", sy, 0)
    yb = swap(yb, "gy", sy, 1)

    ef, hf = pl.pallas_call(
        spread_kernel,
        out_shape=(shape((3, nx, ny + 8, nz), F32), shape((3, nx, ny, nz), F32)),
        in_specs=[HBM, HBM],
        out_specs=[VM, VM],
        scratch_shapes=[
            pltpu.VMEM((3, nx, ny, nz), BF16), pltpu.VMEM((3, nx, ny, nz), BF16),
            pltpu.SemaphoreType.DMA((PARTS,)), pltpu.SemaphoreType.DMA((PARTS,)),
        ],
        compiler_params=params(16),
        name="spread",
    )(adjoint_e, adjoint_h)

    new_e, new_h = pl.pallas_call(
        field_kernel,
        out_shape=(shape(adjoint_e.shape, BF16), shape(adjoint_e.shape, BF16)),
        in_specs=[VM, VM, HBM, SM] + [VM] * 5,
        out_specs=[HBM, HBM],
        scratch_shapes=[
            pltpu.VMEM((nx, ny, nz), I32),
            pltpu.VMEM((3, nx, ny, nz), BF16), pltpu.VMEM((3, nx, ny, nz), BF16),
            pltpu.VMEM((3, nx + 1, ny + 8, nz), F32),
            pltpu.VMEM((2, nx, nz), F32), pltpu.VMEM((2, ny, nz), F32),
        ] + [pltpu.SemaphoreType.DMA((CHUNKS,))] * 3,
        compiler_params=params(20),
        name="fields",
    )(ef, hf, material, inv_eps, xa, xb, ya, yb, y0)

    gradient = pl.pallas_call(
        place_kernel,
        out_shape=shape((DL, 512), F32),
        in_specs=[VM],
        out_specs=VM,
        compiler_params=params(4),
        name="place",
    )(got)
    return new_e, new_h, gradient


def solution(mesh):
    return jax.shard_map(
        per_device,
        mesh=mesh,
        in_specs=(
            P(None, "gx", "gy", None),
            P(None, "gx", "gy", None),
            P("gx", "gy", None),
            P(),
            P(None, "gx", "gy", None),
            P("gx", "gy"),
            P(),
            P(),
        ),
        out_specs=(P(None, "gx", "gy", None), P(None, "gx", "gy", None), P(None, ("gx", "gy"))),
        check_vma=False,
    )
```

time: 36.2 us -> 34.2 us (0.945)
  waiting for transfers between devices: 4.16 us -> 1.77 us
  Pallas kernels: 12.8 us -> 13.2 us
    ppermute x4, waiting for transfers between devices: 4.16 us -> 1.77 us  [swap(): return lax.ppermute(v, axis, pairs)]
    pallas_call x0 -> x1, Pallas kernels: none -> 2.37 us  [per_device(): pl.pallas_call(spread_kernel, out_shape=(shape((3, nx, ny + 8, nz), F32),...]
    pallas_call x1, Pallas kernels: 5.34 us -> 4.21 us  [per_device(): pl.pallas_call(pillar_kernel, out_shape=(shape((256, 128), F32), shape((5...]
    pallas_call x1, Pallas kernels: 5.63 us -> 4.72 us  [per_device(): pl.pallas_call(field_kernel, out_shape=(shape(adjoint_e.shape, BF16), sha...]
  transfers between devices with their start and end apart: 5 -> 5, of which waited for: 1 -> 1; matrix products, arithmetic and copies ran while one was open for 0% -> 0% of each run, Pallas kernels for 30% -> 33%
where the time goes in v3:
time: 34.2 us; the launch traced here: 34 us
  starting transfers between devices  18.2 us (53%)
  Pallas kernels  13.2 us (39%)
  waiting for transfers between devices  1.77 us (5%)
  between operations  0.75 us (2%)
    all_to_all x1, starting transfers between devices, per_device(): got = lax.all_to_all(send.reshape(128, 2, 128), both, 0, 0, tiled=True)  12.6 us
    ppermute x4, starting transfers between devices, swap(): return lax.ppermute(v, axis, pairs)  5.6 us
    pallas_call x1, Pallas kernels, per_device(): pl.pallas_call(field_kernel, out_shape=(shape(adjoint_e.shape, BF16), sha...  4.72 us
    pallas_call x1, Pallas kernels, per_device(): pl.pallas_call(pillar_kernel, out_shape=(shape((256, 128), F32), shape((5...  4.21 us
    pallas_call x1, Pallas kernels, per_device(): pl.pallas_call(spread_kernel, out_shape=(shape((3, nx, ny + 8, nz), F32),...  2.37 us
    ppermute x4, waiting for transfers between devices, swap(): return lax.ppermute(v, axis, pairs)  1.77 us
    pallas_call x1, Pallas kernels, per_device(): pl.pallas_call(place_kernel, out_shape=shape((DL, 512), F32), in_specs=[V...  1.04 us
    pallas_call x1, Pallas kernels, per_device(): pl.pallas_call(face_kernel, out_shape=(shape((5, ny, nz), BF16), shape((5...  0.85 us
  transfers between devices with their start and end apart: 5, of which 1 were waited for; matrix products, arithmetic and copies ran while one was open for 0% of the time, Pallas kernels for 33%

profile of v3, /device:TPU:7, one launch (start us, length us, event | category | flops | bytes accessed | tf_op | source)
XLA Modules:
  0.0 34.0 jit_solution(4530265213171889723)
XLA Ops:
  0.6 0.8 %faces.1 = (bf16[5,64,128]{2,1,0:T(8,128)(2,1)S(1)}, bf16[5,64,128]{2,1,0:T(8,128)(2,1)S(1)}) custom-call(bf16[3,32,64,128]{3,2,1,0:T(8,128)(2,1)} %e_hbm.5, bf16[3,32,64,128]{3,2,1,0:T(8,128)(2,1)} %h_hbm.5), custom_call_target="tpu_custom_call" | custom-call | tf_op jit(solution)/shard_map/faces/pallas_call | solution.py:427
  1.5 1.4 %collective-permute-start = (bf16[5,64,128]{2,1,0:T(8,128)(2,1)S(1)}, bf16[5,64,128]{2,1,0:T(8,128)(2,1)S(1)}, u32[]{:S(2)}, u32[]{:S(2)}) collective-permute-start(bf16[5,64,128]{2,1,0:T(8,128)(2,1)S(1)} %get-tuple-element.15), channel_id=1, source_target_pairs={{0,16},{16,0},{32,48},{48,32},{64,80},{80,64},{96,112},{112,96},{1... | collective-permute-start | bytes 245768 | tf_op jit(solution)/shard_map/ppermute | solution.py:425
  2.9 0.7 %collective-permute-start.1 = (bf16[5,64,128]{2,1,0:T(8,128)(2,1)S(1)}, bf16[5,64,128]{2,1,0:T(8,128)(2,1)S(1)}, u32[]{:S(2)}, u32[]{:S(2)}) collective-permute-start(bf16[5,64,128]{2,1,0:T(8,128)(2,1)S(1)} %get-tuple-element.16), channel_id=1, source_target_pairs={{16,32},{32,16},{48,64},{64,48},{80,96},{96,80},{17,33},{33,17},{4... | collective-permute-start | bytes 245768 | tf_op jit(solution)/shard_map/ppermute | solution.py:425
  3.5 4.2 %pillars.1 = (f32[256,128]{1,0:T(8,128)}, bf16[176,128]{1,0:T(8,128)(2,1)S(1)}, bf16[176,128]{1,0:T(8,128)(2,1)S(1)}, f32[2,32,128]{2,1,0:T(8,128)S(1)}) custom-call(bf16[3,32,64,128]{3,2,1,0:T(8,128)(2,1)} %e_hbm.5, bf16[3,32,64,128]{3,2,1,0:T(8,128)(2,1)} %h_hbm.5, bf16[3,32,64,128]{3,2,1,0:T(8,128)(2,1)} %f_hbm.1, s32[32,64]{1,0:T(8,128)} %slot_hbm.1, ...), custom_call_target="tpu_custom_call" | custom-call | tf_op jit(solution)/shard_map/pillars/pallas_call | solution.py:438
  7.7 12.6 %all-to-all-start = ((f32[128,2,128]{2,1,0:T(2,128)}), f32[128,2,128]{2,1,0:T(2,128)S(1)}, u32[]{:S(2)}, u32[]{:S(2)}) async-start(f32[128,2,128]{2,1,0:T(2,128)} %bitcast.3), calls=%async_computation | async-start | bytes 262144 | tf_op jit(solution)/shard_map/all_to_all | solution.py:461
  20.4 0.0 collective-permute-done.xa_ref
  20.4 0.0 collective-permute-done.1.xb_ref
  20.5 3.5 %collective-permute-start.3 = (bf16[176,128]{1,0:T(8,128)(2,1)S(1)}, bf16[176,128]{1,0:T(8,128)(2,1)S(1)}, u32[]{:S(2)}, u32[]{:S(2)}) collective-permute-start(bf16[176,128]{1,0:T(8,128)(2,1)S(1)} %dynamic_update_slice.7), channel_id=1, source_target_pairs={{1,2},{2,1},{3,4},{4,3},{5,6},{6,5},{7,8},{8,7},{9,10},{10,9},{11,... | collective-permute-start | bytes 135176 | tf_op jit(solution)/shard_map/ppermute | solution.py:425
  24.0 0.0 copy-start
  24.0 0.1 collective-permute-start.2
  24.1 2.4 %spread.1 = (f32[3,32,72,128]{3,2,1,0:T(8,128)S(1)}, f32[3,32,64,128]{3,2,1,0:T(8,128)S(1)}) custom-call(bf16[3,32,64,128]{3,2,1,0:T(8,128)(2,1)} %e_hbm.5, bf16[3,32,64,128]{3,2,1,0:T(8,128)(2,1)} %h_hbm.5), custom_call_target="tpu_custom_call" | custom-call | tf_op jit(solution)/shard_map/spread/pallas_call | solution.py:472
  26.5 1.8 %collective-permute-done.3.yb_ref = bf16[176,128]{1,0:T(8,128)(2,1)S(1)} collective-permute-done((bf16[176,128]{1,0:T(8,128)(2,1)S(1)}, bf16[176,128]{1,0:T(8,128)(2,1)S(1)}, u32[]{:S(2)}, u32[]{:S(2)}) %collective-permute-start.3) | collective-permute-done | bytes 45088 | tf_op jit(solution)/shard_map/ppermute | solution.py:425
  28.2 0.0 collective-permute-done.2.ya_ref
  28.2 0.0 copy-done
  28.2 4.7 %fields.1 = (bf16[3,32,64,128]{3,2,1,0:T(8,128)(2,1)}, bf16[3,32,64,128]{3,2,1,0:T(8,128)(2,1)}) custom-call(f32[3,32,72,128]{3,2,1,0:T(8,128)S(1)} %get-tuple-element.13.ef, f32[3,32,64,128]{3,2,1,0:T(8,128)S(1)} %get-tuple-element.14.hf, s32[32,64,128]{2,1,0:T(8,128)} %m_hbm.1, f32[4]{0:T(128)S(1)} %copy-done, ...), custom_call_target="tpu_custom_call" | custom-call | tf_op jit(solution)/shard_map/fields/pallas_call | solution.py:485
  33.0 0.0 all-to-all-done
  33.0 1.0 %place.1 = f32[32,512]{1,0:T(8,128)} custom-call(f32[256,128]{1,0:T(8,128)S(1)} %bitcast.7), custom_call_target="tpu_custom_call" | custom-call | tf_op jit(solution)/shard_map/place/pallas_call | solution.py:500
  (3 shorter events, 0.1 us)
Async XLA Ops:
  1.5 18.9 %collective-permute-start = (bf16[5,64,128]{2,1,0:T(8,128)(2,1)S(1)}, bf16[5,64,128]{2,1,0:T(8,128)(2,1)S(1)}, u32[]{:S(2)}, u32[]{:S(2)}) collective-permute-start(bf16[5,64,128]{2,1,0:T(8,128)(2,1)S(1)} %get-tuple-element.15), channel_id=1, source_target_pairs={{0,16},{16,0},{32,48},{48,32},{64,80},{80,64},{96,112},{112,96},{1... | collective-permute-start | bytes 245768 | tf_op jit(solution)/shard_map/ppermute | solution.py:425
  2.9 17.5 %collective-permute-start.1 = (bf16[5,64,128]{2,1,0:T(8,128)(2,1)S(1)}, bf16[5,64,128]{2,1,0:T(8,128)(2,1)S(1)}, u32[]{:S(2)}, u32[]{:S(2)}) collective-permute-start(bf16[5,64,128]{2,1,0:T(8,128)(2,1)S(1)} %get-tuple-element.16), channel_id=1, source_target_pairs={{16,32},{32,16},{48,64},{64,48},{80,96},{96,80},{17,33},{33,17},{4... | collective-permute-start | bytes 245768 | tf_op jit(solution)/shard_map/ppermute | solution.py:425
  7.7 25.2 %all-to-all-start = ((f32[128,2,128]{2,1,0:T(2,128)}), f32[128,2,128]{2,1,0:T(2,128)S(1)}, u32[]{:S(2)}, u32[]{:S(2)}) async-start(f32[128,2,128]{2,1,0:T(2,128)} %bitcast.3), calls=%async_computation | async-start | bytes 262144 | tf_op jit(solution)/shard_map/all_to_all | solution.py:461
  20.5 7.8 %collective-permute-start.3 = (bf16[176,128]{1,0:T(8,128)(2,1)S(1)}, bf16[176,128]{1,0:T(8,128)(2,1)S(1)}, u32[]{:S(2)}, u32[]{:S(2)}) collective-permute-start(bf16[176,128]{1,0:T(8,128)(2,1)S(1)} %dynamic_update_slice.7), channel_id=1, source_target_pairs={{1,2},{2,1},{3,4},{4,3},{5,6},{6,5},{7,8},{8,7},{9,10},{10,9},{11,... | collective-permute-start | bytes 135176 | tf_op jit(solution)/shard_map/ppermute | solution.py:425
  24.0 4.2 %copy-start = (f32[4]{0:T(128)S(1)}, f32[4]{0:T(128)}, u32[]{:S(2)}) copy-start(f32[4]{0:T(128)} %eps_ref.1) | copy-start | bytes 52
  24.0 4.2 %collective-permute-start.2 = (bf16[176,128]{1,0:T(8,128)(2,1)S(1)}, bf16[176,128]{1,0:T(8,128)(2,1)S(1)}, u32[]{:S(2)}, u32[]{:S(2)}) collective-permute-start(bf16[176,128]{1,0:T(8,128)(2,1)S(1)} %dynamic_update_slice.6), channel_id=1, source_target_pairs={{0,1},{1,0},{2,3},{3,2},{4,5},{5,4},{6,7},{7,6},{8,9},{9,8},{10,11... | collective-permute-start | bytes 135176 | tf_op jit(solution)/shard_map/ppermute | solution.py:425

commit v4 on v3

--- a/solution.py
+++ b/solution.py
@@ -63,9 +63,9 @@
 
 
 def pillar_kernel(
-    e_hbm, h_hbm, f_hbm, slot_hbm, tiles_hbm, rank_hbm,
-    send_ref, ya_ref, yb_ref, y0_ref,
-    e, f, y_first, y_last, y_h, tiles, rank, slot, cells, ids, acc, sem, fsem, msem,
+    e_hbm, h_hbm, m_hbm, f_hbm, slot_hbm, tiles_hbm, rank_hbm,
+    send_ref, ya_ref, yb_ref, y0_ref, e, m,
+    f, y_first, y_last, y_h, tiles, rank, slot, cells, ids, acc, sem, fsem, msem,
 ):
     gx, gy = lax.axis_index("gx"), lax.axis_index("gy")
     _, nx, ny, nz = e.shape
@@ -86,17 +86,18 @@
         pltpu.make_async_copy(e_hbm.at[:, :, pl.ds(ny - 8, 8)], y_last, msem.at[4]),
         pltpu.make_async_copy(h_hbm.at[0, :, pl.ds(ny - 8, 8)], y_h.at[0], msem.at[5]),
         pltpu.make_async_copy(h_hbm.at[2, :, pl.ds(ny - 8, 8)], y_h.at[1], msem.at[6]),
+        pltpu.make_async_copy(m_hbm, m, msem.at[7]),
     ]
     for one in extra[:3]:
         one.start()
     for one, two in copies[:1]:
         one.start()
         two.start()
-    for one in extra[3:]:
-        one.start()
     for one, two in copies[1:]:
         one.start()
         two.start()
+    for one in extra[3:]:
+        one.start()
     ids[...] = iota(ids.shape, 0)
     lanes, rows = iota((128, 128), 1), iota((128, 128), 0)
 
@@ -184,7 +185,7 @@
         values = values + dot(hi, gather) + dot(lo, gather)
     send_ref[pl.ds(0, 128, stride=2), :] = values
 
-    for one in extra[3:]:
+    for one in extra[3:7]:
         one.wait()
     at = iota((nx, 8 * nx), 1) - 8 * iota((nx, 8 * nx), 0)
     low = jnp.where(at == 0, 1.0, 0.0).astype(BF16)
@@ -217,6 +218,9 @@
     def _():
         pack(yb_ref, ya_ref)
 
+    for one in extra[7:]:
+        one.wait()
+
 
 def eye_like(distance, n):
     return jnp.where(iota((n, n), 0) == iota((n, n), 1) + distance, 1.0, 0.0)
@@ -232,28 +236,29 @@
     return jnp.concatenate([one.reshape(shape), two.reshape(shape)], axis=1)
 
 
-def spread_kernel(e_hbm, h_hbm, ef_ref, hf_ref, e, h, sem, hsem):
-    _, nx, ny, nz = h.shape
-    parts = sem.shape[0]
-    step = nx // parts
+def spread_kernel(e, h_hbm, m, eps_ref, ef_ref, hf_ref, cf_ref, h, sem):
+    nx, ny, nz = m.shape
+    step = nx // PARTS
     loads = []
-    for i in range(parts):
+    for i in range(PARTS):
         part = pl.ds(i * step, step)
-        loads.append((
-            pltpu.make_async_copy(e_hbm.at[:, part], e.at[:, part], sem.at[i]),
-            pltpu.make_async_copy(h_hbm.at[:, part], h.at[:, part], hsem.at[i]),
-        ))
-    for group in loads:
-        for one in group:
-            one.start()
+        loads.append(pltpu.make_async_copy(h_hbm.at[:, part], h.at[:, part], sem.at[i]))
+    for one in loads:
+        one.start()
+    values = [0.25 * eps_ref[k] for k in range(4)]
     eye = eye_like(0, nz)
     ahead = eye_like(1, nz) - eye
     none = jnp.zeros((nz, nz), F32)
     wx = square(2.0 * eye, none, ahead, eye)
     wy = square(2.0 * eye, none, -ahead, eye)
-    for i in range(parts):
-        for one in loads[i]:
-            one.wait()
+    for x in range(nx):
+        kind = m[x]
+        cf_ref[x] = jnp.where(
+            kind < 2, jnp.where(kind == 0, values[0], values[1]), jnp.where(kind == 2, values[2], values[3])
+        )
+        ef_ref[2, x, pl.ds(0, ny)] = e[2, x].astype(F32)
+    for i in range(PARTS):
+        loads[i].wait()
         part = pl.ds(i * step, step)
         for c, other, w in ((0, 1, wx), (1, 0, wy)):
             both = dot(side(h[c, part], e[other, part]), w)
@@ -266,28 +271,24 @@
             x = i * step + k
             hz = h[2, x].astype(F32)
             hf_ref[2, x] = hz + hz
-            ef_ref[2, x, pl.ds(0, ny)] = e[2, x].astype(F32)
 
 
 def field_kernel(
-    ef, hf, m_hbm, eps_ref, xa_ref, xb_ref, ya_ref, yb_ref, y0_ref,
+    ef, hf, cf, xa_ref, xb_ref, ya_ref, yb_ref, y0_ref,
     ne_hbm, nh_hbm,
-    m, ne, nh, gf, high, beyond, msem, esem, osem,
+    ne, nh, gf, bz, high, beyond, esem, osem,
 ):
     gx, gy = lax.axis_index("gx"), lax.axis_index("gy")
-    nx, ny, nz = m.shape
-    parts = msem.shape[0]
+    nx, ny, nz = cf.shape
+    parts = esem.shape[0]
     step = nx // parts
-    loads, stores = [], []
+    stores = []
     for i in range(parts):
         part = pl.ds(i * step, step)
-        loads.append(pltpu.make_async_copy(m_hbm.at[part], m.at[part], msem.at[i]))
         stores.append((
             pltpu.make_async_copy(nh.at[:, part], nh_hbm.at[:, part], osem.at[i]),
             pltpu.make_async_copy(ne.at[:, part], ne_hbm.at[:, part], esem.at[i]),
         ))
-    for one in loads:
-        one.start()
 
     even_x, even_y = gx % 2 == 0, gy % 2 == 0
     rows, kept = pl.ds(0, ny), pl.ds(8, ny)
@@ -328,10 +329,6 @@
     back = 2.0 * (eye_like(0, nz) - eye_like(-1, nz))
     none = jnp.zeros((nz, nz), F32)
     wb = square(back, none, none, back)
-    lane = iota((ny, nz), 1)
-    table = jnp.zeros((ny, nz), F32)
-    for k in range(4):
-        table = jnp.where(lane == k, 0.25 * eps_ref[k], table)
     seventh = iota((8, nz), 0) == 7
 
     def up_y(c, which, x):
@@ -350,33 +347,30 @@
             nh[c, x] = g * BF16(0.5)
             gf[c, x + 1, kept] = g.astype(F32)
 
-    picks = lax.GatherDimensionNumbers(
-        offset_dims=(), collapsed_slice_dims=(1,), start_index_map=(1,),
-        operand_batching_dims=(0,), start_indices_batching_dims=(0,),
-    )
-
-    def second(x, along):
+    def second(x):
         shifted = pl.ds(7, ny)
         gx_, gy_, gz_ = [gf[c, x + 1, kept] for c in range(3)]
-        coef = lax.gather(
-            table, m[x][..., None], picks, (1, 1), mode=lax.GatherScatterMode.PROMISE_IN_BOUNDS
-        )
-        tx = (gz_ - gf[2, x + 1, shifted]) - along[:, nz:]
-        ty = along[:, :nz] - (gz_ - gf[2, x, kept])
+        slot = pl.ds(x % (2 * step) * ny, ny)
+        tx = (gz_ - gf[2, x + 1, shifted]) - bz[1, slot]
+        ty = bz[0, slot] - (gz_ - gf[2, x, kept])
         tz = (gy_ - gf[1, x, kept]) - (gx_ - gf[0, x + 1, shifted])
+        coef = cf[x]
         for c, t in enumerate((tx, ty, tz)):
             ne[c, x] = (ef[c, x, rows] + coef * t).astype(BF16)
 
     for i in range(parts + 1):
-        if i > 0:
-            loads[i - 1].wait()
-            part = pl.ds((i - 1) * step, step)
-            along = dot(side(nh[0, part], nh[1, part]), wb)
         for k in range(step):
             if i < parts:
                 first(i * step + k)
+        if i < parts:
+            part = pl.ds(i * step, step)
+            both = dot(side(nh[0, part], nh[1, part]), wb)
+            slot = pl.ds(i % 2 * step * ny, step * ny)
+            bz[0, slot] = both[:, :nz]
+            bz[1, slot] = both[:, nz:]
+        for k in range(step):
             if i > 0:
-                second((i - 1) * step + k, along[k * ny : (k + 1) * ny])
+                second((i - 1) * step + k)
         if i < parts:
             stores[i][0].start()
         if i > 0:
@@ -435,28 +429,29 @@
     )(adjoint_e, adjoint_h)
     xa, xb = swap(xa, "gx", sx, 0), swap(xb, "gx", sx, 1)
 
-    send, ya, yb, y0 = pl.pallas_call(
+    send, ya, yb, y0, e_vm, m_vm = pl.pallas_call(
         pillar_kernel,
         out_shape=(
             shape((256, 128), F32),
             shape((5 * nx + 16, nz), BF16), shape((5 * nx + 16, nz), BF16),
             shape((2, nx, nz), F32),
+            shape(adjoint_e.shape, BF16), shape((nx, ny, nz), I32),
         ),
-        in_specs=[HBM] * 6,
-        out_specs=[VM] * 4,
+        in_specs=[HBM] * 7,
+        out_specs=[VM] * 6,
         scratch_shapes=[
-            pltpu.VMEM((3, nx, ny, nz), BF16), pltpu.VMEM((3, nx, ny, nz), BF16),
+            pltpu.VMEM((3, nx, ny, nz), BF16),
             pltpu.VMEM((3, nx, 8, nz), BF16), pltpu.VMEM((3, nx, 8, nz), BF16),
             pltpu.VMEM((2, nx, 8, nz), BF16),
             pltpu.VMEM((8, 512), I32), pltpu.VMEM((64, 128), I32), pltpu.VMEM((nx, ny), I32),
             pltpu.VMEM((nx, 2 * ny), I32), pltpu.VMEM((512, 128), I32),
             pltpu.VMEM((512, 2 * nz), F32),
             pltpu.SemaphoreType.DMA((PARTS,)), pltpu.SemaphoreType.DMA((PARTS,)),
-            pltpu.SemaphoreType.DMA((7,)),
+            pltpu.SemaphoreType.DMA((8,)),
         ],
         compiler_params=params(12),
         name="pillars",
-    )(adjoint_e, adjoint_h, forward_design, cell_slot, tile_pillars, ranks)
+    )(adjoint_e, adjoint_h, material, forward_design, cell_slot, tile_pillars, ranks)
 
     got = lax.all_to_all(send.reshape(128, 2, 128), both, 0, 0, tiled=True)
     got = got.reshape(256, 128)
@@ -469,33 +464,32 @@
     ya = swap(ya, "gy", sy, 0)
     yb = swap(yb, "gy", sy, 1)
 
-    ef, hf = pl.pallas_call(
+    ef, hf, cf = pl.pallas_call(
         spread_kernel,
-        out_shape=(shape((3, nx, ny + 8, nz), F32), shape((3, nx, ny, nz), F32)),
-        in_specs=[HBM, HBM],
-        out_specs=[VM, VM],
-        scratch_shapes=[
-            pltpu.VMEM((3, nx, ny, nz), BF16), pltpu.VMEM((3, nx, ny, nz), BF16),
-            pltpu.SemaphoreType.DMA((PARTS,)), pltpu.SemaphoreType.DMA((PARTS,)),
-        ],
+        out_shape=(
+            shape((3, nx, ny + 8, nz), F32), shape((3, nx, ny, nz), F32), shape((nx, ny, nz), F32)
+        ),
+        in_specs=[VM, HBM, VM, SM],
+        out_specs=[VM] * 3,
+        scratch_shapes=[pltpu.VMEM((3, nx, ny, nz), BF16), pltpu.SemaphoreType.DMA((PARTS,))],
         compiler_params=params(16),
         name="spread",
-    )(adjoint_e, adjoint_h)
+    )(e_vm, adjoint_h, m_vm, inv_eps)
 
     new_e, new_h = pl.pallas_call(
         field_kernel,
         out_shape=(shape(adjoint_e.shape, BF16), shape(adjoint_e.shape, BF16)),
-        in_specs=[VM, VM, HBM, SM] + [VM] * 5,
+        in_specs=[VM] * 8,
         out_specs=[HBM, HBM],
         scratch_shapes=[
-            pltpu.VMEM((nx, ny, nz), I32),
             pltpu.VMEM((3, nx, ny, nz), BF16), pltpu.VMEM((3, nx, ny, nz), BF16),
             pltpu.VMEM((3, nx + 1, ny + 8, nz), F32),
+            pltpu.VMEM((2, 2 * nx // CHUNKS * ny, nz), F32),
             pltpu.VMEM((2, nx, nz), F32), pltpu.VMEM((2, ny, nz), F32),
-        ] + [pltpu.SemaphoreType.DMA((CHUNKS,))] * 3,
+        ] + [pltpu.SemaphoreType.DMA((CHUNKS,))] * 2,
         compiler_params=params(20),
         name="fields",
-    )(ef, hf, material, inv_eps, xa, xb, ya, yb, y0)
+    )(ef, hf, cf, xa, xb, ya, yb, y0)
 
     gradient = pl.pallas_call(
         place_kernel,

time: 34.2 us -> 32.5 us (0.950)
  the two profiles are of different devices: /device:TPU:7 before, /device:TPU:1 now
where the time goes in v4:
time: 32.5 us; the launch traced here: 32.2 us
  starting transfers between devices  19 us (58%)
  Pallas kernels  11.5 us (35%)
  waiting for transfers between devices  0.86 us (3%)
  between operations  0.77 us (2%)
    all_to_all x1, starting transfers between devices, per_device(): got = lax.all_to_all(send.reshape(128, 2, 128), both, 0, 0, tiled=True)  12.5 us
    ppermute x4, starting transfers between devices, swap(): return lax.ppermute(v, axis, pairs)  6.46 us
    pallas_call x1, Pallas kernels, per_device(): pl.pallas_call(pillar_kernel, out_shape=(shape((256, 128), F32), shape((5...  4.07 us
    pallas_call x1, Pallas kernels, per_device(): pl.pallas_call(field_kernel, out_shape=(shape(adjoint_e.shape, BF16), sha...  2.8 us
    pallas_call x1, Pallas kernels, per_device(): pl.pallas_call(spread_kernel, out_shape=(shape((3, nx, ny + 8, nz), F32),...  2.77 us
    pallas_call x1, Pallas kernels, per_device(): pl.pallas_call(place_kernel, out_shape=shape((DL, 512), F32), in_specs=[V...  1.03 us
    all_to_all x1, waiting for transfers between devices, per_device(): got = lax.all_to_all(send.reshape(128, 2, 128), both, 0, 0, tiled=True)  0.85 us
    pallas_call x1, Pallas kernels, per_device(): pl.pallas_call(face_kernel, out_shape=(shape((5, ny, nz), BF16), shape((5...  0.85 us
  transfers between devices with their start and end apart: 5, of which 1 were waited for; matrix products, arithmetic and copies ran while one was open for 0% of the time, Pallas kernels for 30%

profile of v4, /device:TPU:1, one launch (start us, length us, event | category | flops | bytes accessed | tf_op | source)
XLA Modules:
  0.0 32.2 jit_solution(5643264995738917193)
XLA Ops:
  0.6 0.8 %faces.1 = (bf16[5,64,128]{2,1,0:T(8,128)(2,1)S(1)}, bf16[5,64,128]{2,1,0:T(8,128)(2,1)S(1)}) custom-call(bf16[3,32,64,128]{3,2,1,0:T(8,128)(2,1)} %e_hbm.3, bf16[3,32,64,128]{3,2,1,0:T(8,128)(2,1)} %h_hbm.5), custom_call_target="tpu_custom_call" | custom-call | tf_op jit(solution)/shard_map/faces/pallas_call | solution.py:421
  1.5 2.2 %collective-permute-start = (bf16[5,64,128]{2,1,0:T(8,128)(2,1)S(1)}, bf16[5,64,128]{2,1,0:T(8,128)(2,1)S(1)}, u32[]{:S(2)}, u32[]{:S(2)}) collective-permute-start(bf16[5,64,128]{2,1,0:T(8,128)(2,1)S(1)} %get-tuple-element.21), channel_id=1, source_target_pairs={{0,16},{16,0},{32,48},{48,32},{64,80},{80,64},{96,112},{112,96},{1... | collective-permute-start | bytes 245768 | tf_op jit(solution)/shard_map/ppermute | solution.py:419
  3.7 0.7 %collective-permute-start.1 = (bf16[5,64,128]{2,1,0:T(8,128)(2,1)S(1)}, bf16[5,64,128]{2,1,0:T(8,128)(2,1)S(1)}, u32[]{:S(2)}, u32[]{:S(2)}) collective-permute-start(bf16[5,64,128]{2,1,0:T(8,128)(2,1)S(1)} %get-tuple-element.22), channel_id=1, source_target_pairs={{16,32},{32,16},{48,64},{64,48},{80,96},{96,80},{17,33},{33,17},{4... | collective-permute-start | bytes 245768 | tf_op jit(solution)/shard_map/ppermute | solution.py:419
  4.3 0.0 copy-start
  4.4 4.1 %pillars.1 = (f32[256,128]{1,0:T(8,128)}, bf16[176,128]{1,0:T(8,128)(2,1)S(1)}, bf16[176,128]{1,0:T(8,128)(2,1)S(1)}, f32[2,32,128]{2,1,0:T(8,128)S(1)}, bf16[3,...) custom-call(bf16[3,32,64,128]{3,2,1,0:T(8,128)(2,1)} %e_hbm.3, bf16[3,32,64,128]{3,2,1,0:T(8,128)(2,1)} %h_hbm.5, ...), custom_call_target="tpu_custom_call" | custom-call | tf_op jit(solution)/shard_map/pillars/pallas_call | solution.py:432
  8.4 12.5 %all-to-all-start = ((f32[128,2,128]{2,1,0:T(2,128)}), f32[128,2,128]{2,1,0:T(2,128)S(1)}, u32[]{:S(2)}, u32[]{:S(2)}) async-start(f32[128,2,128]{2,1,0:T(2,128)} %bitcast.3), calls=%async_computation | async-start | bytes 262144 | tf_op jit(solution)/shard_map/all_to_all | solution.py:456
  21.0 0.0 collective-permute-done.xa_ref
  21.0 0.0 collective-permute-done.1.xb_ref
  21.1 3.5 %collective-permute-start.3 = (bf16[176,128]{1,0:T(8,128)(2,1)S(1)}, bf16[176,128]{1,0:T(8,128)(2,1)S(1)}, u32[]{:S(2)}, u32[]{:S(2)}) collective-permute-start(bf16[176,128]{1,0:T(8,128)(2,1)S(1)} %dynamic_update_slice.7), channel_id=1, source_target_pairs={{1,2},{2,1},{3,4},{4,3},{5,6},{6,5},{7,8},{8,7},{9,10},{10,9},{11,... | collective-permute-start | bytes 135176 | tf_op jit(solution)/shard_map/ppermute | solution.py:419
  24.6 0.1 collective-permute-start.2
  24.7 0.0 copy-done
  24.7 2.8 %spread.1 = (f32[3,32,72,128]{3,2,1,0:T(8,128)S(1)}, f32[3,32,64,128]{3,2,1,0:T(8,128)S(1)}, f32[32,64,128]{2,1,0:T(8,128)S(1)}) custom-call(bf16[3,32,64,128]{3,2,1,0:T(8,128)(2,1)S(1)} %get-tuple-element.16.e, bf16[3,32,64,128]{3,2,1,0:T(8,128)(2,1)} %h_hbm.5, s32[32,64,128]{2,1,0:T(8,128)S(1)} %get-tuple-element.17.m, f32[4]{0:T(128)S(1)} %copy-done), custom_call_target="tpu_custom_call" | custom-call | tf_op jit(solution)/shard_map/spread/pallas_call | solution.py:467
  27.5 0.0 collective-permute-done.3.yb_ref
  27.5 0.0 collective-permute-done.2.ya_ref
  27.5 2.8 %fields.1 = (bf16[3,32,64,128]{3,2,1,0:T(8,128)(2,1)}, bf16[3,32,64,128]{3,2,1,0:T(8,128)(2,1)}) custom-call(f32[3,32,72,128]{3,2,1,0:T(8,128)S(1)} %get-tuple-element.18.ef, f32[3,32,64,128]{3,2,1,0:T(8,128)S(1)} %get-tuple-element.19.hf, f32[32,64,128]{2,1,0:T(8,128)S(1)} %get-tuple-element.20.cf, bf16[5,64,128]{2,1,0:T(8,128)(2,1)S(1)} %collective-permute-done.xa_ref, ...), custom_call_target="tpu_custom_call" | custom-call | tf_op jit(solution)/shard_map/fields/pallas_call | solution.py:479
  30.3 0.9 %all-to-all-done = f32[128,2,128]{2,1,0:T(2,128)S(1)} async-done(((f32[128,2,128]{2,1,0:T(2,128)}), f32[128,2,128]{2,1,0:T(2,128)S(1)}, u32[]{:S(2)}, u32[]{:S(2)}) %all-to-all-start) | async-done | bytes 131104 | tf_op jit(solution)/shard_map/all_to_all | solution.py:456
  31.2 1.0 %place.1 = f32[32,512]{1,0:T(8,128)} custom-call(f32[256,128]{1,0:T(8,128)S(1)} %bitcast.7), custom_call_target="tpu_custom_call" | custom-call | tf_op jit(solution)/shard_map/place/pallas_call | solution.py:494
  (3 shorter events, 0.1 us)
Async XLA Ops:
  1.5 19.5 %collective-permute-start = (bf16[5,64,128]{2,1,0:T(8,128)(2,1)S(1)}, bf16[5,64,128]{2,1,0:T(8,128)(2,1)S(1)}, u32[]{:S(2)}, u32[]{:S(2)}) collective-permute-start(bf16[5,64,128]{2,1,0:T(8,128)(2,1)S(1)} %get-tuple-element.21), channel_id=1, source_target_pairs={{0,16},{16,0},{32,48},{48,32},{64,80},{80,64},{96,112},{112,96},{1... | collective-permute-start | bytes 245768 | tf_op jit(solution)/shard_map/ppermute | solution.py:419
  3.7 17.3 %collective-permute-start.1 = (bf16[5,64,128]{2,1,0:T(8,128)(2,1)S(1)}, bf16[5,64,128]{2,1,0:T(8,128)(2,1)S(1)}, u32[]{:S(2)}, u32[]{:S(2)}) collective-permute-start(bf16[5,64,128]{2,1,0:T(8,128)(2,1)S(1)} %get-tuple-element.22), channel_id=1, source_target_pairs={{16,32},{32,16},{48,64},{64,48},{80,96},{96,80},{17,33},{33,17},{4... | collective-permute-start | bytes 245768 | tf_op jit(solution)/shard_map/ppermute | solution.py:419
  4.3 20.4 %copy-start = (f32[4]{0:T(128)S(1)}, f32[4]{0:T(128)}, u32[]{:S(2)}) copy-start(f32[4]{0:T(128)} %eps_ref.1) | copy-start | bytes 52
  8.4 22.8 %all-to-all-start = ((f32[128,2,128]{2,1,0:T(2,128)}), f32[128,2,128]{2,1,0:T(2,128)S(1)}, u32[]{:S(2)}, u32[]{:S(2)}) async-start(f32[128,2,128]{2,1,0:T(2,128)} %bitcast.3), calls=%async_computation | async-start | bytes 262144 | tf_op jit(solution)/shard_map/all_to_all | solution.py:456
  21.1 6.5 %collective-permute-start.3 = (bf16[176,128]{1,0:T(8,128)(2,1)S(1)}, bf16[176,128]{1,0:T(8,128)(2,1)S(1)}, u32[]{:S(2)}, u32[]{:S(2)}) collective-permute-start(bf16[176,128]{1,0:T(8,128)(2,1)S(1)} %dynamic_update_slice.7), channel_id=1, source_target_pairs={{1,2},{2,1},{3,4},{4,3},{5,6},{6,5},{7,8},{8,7},{9,10},{10,9},{11,... | collective-permute-start | bytes 135176 | tf_op jit(solution)/shard_map/ppermute | solution.py:419
  24.6 2.9 %collective-permute-start.2 = (bf16[176,128]{1,0:T(8,128)(2,1)S(1)}, bf16[176,128]{1,0:T(8,128)(2,1)S(1)}, u32[]{:S(2)}, u32[]{:S(2)}) collective-permute-start(bf16[176,128]{1,0:T(8,128)(2,1)S(1)} %dynamic_update_slice.6), channel_id=1, source_target_pairs={{0,1},{1,0},{2,3},{3,2},{4,5},{5,4},{6,7},{7,6},{8,9},{9,8},{10,11... | collective-permute-start | bytes 135176 | tf_op jit(solution)/shard_map/ppermute | solution.py:419

commit v5 on v4

--- a/solution.py
+++ b/solution.py
@@ -25,31 +25,6 @@
 
 def dot(a, b):
     return jnp.dot(a, b, preferred_element_type=F32)
-
-
-def face_kernel(e_hbm, h_hbm, a_ref, b_ref, sem):
-    gx = lax.axis_index("gx")
-    last = e_hbm.shape[1] - 1
-
-    def fill(up_ref, down_ref):
-        copies = [
-            pltpu.make_async_copy(e_hbm.at[:, last], up_ref.at[pl.ds(0, 3)], sem.at[0]),
-            pltpu.make_async_copy(h_hbm.at[pl.ds(1, 2), last], up_ref.at[pl.ds(3, 2)], sem.at[1]),
-            pltpu.make_async_copy(e_hbm.at[pl.ds(1, 2), 0], down_ref.at[pl.ds(0, 2)], sem.at[2]),
-        ]
-        for one in copies:
-            one.start()
-        down_ref[pl.ds(2, 3)] = jnp.zeros((3,) + down_ref.shape[1:], BF16)
-        for one in copies:
-            one.wait()
-
-    @pl.when(gx % 2 == 0)
-    def _():
-        fill(a_ref, b_ref)
-
-    @pl.when(gx % 2 == 1)
-    def _():
-        fill(b_ref, a_ref)
 
 
 def lookup(table, index):
@@ -64,8 +39,8 @@
 
 def pillar_kernel(
     e_hbm, h_hbm, m_hbm, f_hbm, slot_hbm, tiles_hbm, rank_hbm,
-    send_ref, ya_ref, yb_ref, y0_ref, e, m,
-    f, y_first, y_last, y_h, tiles, rank, slot, cells, ids, acc, sem, fsem, msem,
+    sent_ref, xa_ref, xb_ref, ya_ref, yb_ref, y0_ref, e, m,
+    send_ref, f, y_first, y_last, y_h, tiles, rank, slot, cells, ids, acc, sem, fsem, msem, xsem,
 ):
     gx, gy = lax.axis_index("gx"), lax.axis_index("gy")
     _, nx, ny, nz = e.shape
@@ -98,6 +73,26 @@
         two.start()
     for one in extra[3:]:
         one.start()
+
+    def faces(up_ref, down_ref):
+        return [
+            pltpu.make_async_copy(e_hbm.at[:, nx - 1], up_ref.at[pl.ds(0, 3)], xsem.at[0]),
+            pltpu.make_async_copy(h_hbm.at[pl.ds(1, 2), nx - 1], up_ref.at[pl.ds(3, 2)], xsem.at[1]),
+            pltpu.make_async_copy(e_hbm.at[pl.ds(1, 2), 0], down_ref.at[pl.ds(0, 2)], xsem.at[2]),
+        ]
+
+    @pl.when(gx % 2 == 0)
+    def _():
+        for one in faces(xa_ref, xb_ref):
+            one.start()
+        xb_ref[pl.ds(2, 3)] = jnp.zeros((3, ny, nz), BF16)
+
+    @pl.when(gx % 2 == 1)
+    def _():
+        for one in faces(xb_ref, xa_ref):
+            one.start()
+        xa_ref[pl.ds(2, 3)] = jnp.zeros((3, ny, nz), BF16)
+
     ids[...] = iota(ids.shape, 0)
     lanes, rows = iota((128, 128), 1), iota((128, 128), 0)
 
@@ -141,7 +136,7 @@
         jnp.concatenate(ones, axis=1), jnp.concatenate(spots, axis=1),
         (((1,), (1,)), ((), ())), preferred_element_type=F32,
     )
-    send_ref[pl.ds(1, 128, stride=2), :] = jnp.concatenate([spots, jnp.zeros((128, 112), F32)], axis=1)
+    send_ref[pl.ds(2, 128, stride=4), :] = jnp.concatenate([spots, jnp.zeros((128, 112), F32)], axis=1)
     target = jnp.concatenate([turn[q] * 128 + owner[q] for q in range(4)], axis=0)
     own = jnp.sum(jnp.where(iota(tiles.shape, 0) == gy % 8, tiles[...], 0), axis=0, keepdims=True)
     own = jnp.concatenate([own[:, 128 * q : 128 * (q + 1)] for q in range(4)], axis=0)
@@ -183,7 +178,9 @@
         hi, lo = split(part[:, :nz] + part[:, nz:])
         gather = jnp.where(lanes == 32 * k + (rows >> 2), 0.125, 0.0).astype(BF16)
         values = values + dot(hi, gather) + dot(lo, gather)
-    send_ref[pl.ds(0, 128, stride=2), :] = values
+    hi, lo = split(values)
+    send_ref[pl.ds(0, 128, stride=4), :] = hi.astype(F32)
+    send_ref[pl.ds(1, 128, stride=4), :] = lo.astype(F32)
 
     for one in extra[3:7]:
         one.wait()
@@ -200,6 +197,19 @@
     up_y = face(high, y_last[0], y_last[1]) + face(high, y_last[2], y_h[0]) + face(high, y_h[1], y_h[1])[:1]
     y0_ref[0] = y0x
     y0_ref[1] = y0z
+
+    sx, sy = lax.axis_size("gx"), lax.axis_size("gy")
+    send_ref[pl.ds(3, 128, stride=4), :] = jnp.zeros((128, nz), F32)
+
+    @pl.when((gx < sx - 1) & (gy > 0))
+    def _():
+        send_ref[pl.ds(4 * ((gx + 1) * sy + gy - 1) + 3, 1), :] = y0x[nx - 1 :]
+
+    @pl.when((gx > 0) & (gy < sy - 1))
+    def _():
+        send_ref[pl.ds(4 * ((gx - 1) * sy + gy + 1) + 3, 1), :] = up_y[1][:1]
+
+    sent_ref[...] = send_ref[...].astype(BF16)
 
     def pack(up_ref, down_ref):
         for c in range(5):
@@ -207,8 +217,6 @@
         down_ref[pl.ds(0, nx)] = y0x.astype(BF16)
         down_ref[pl.ds(nx, nx)] = y0z.astype(BF16)
         down_ref[pl.ds(2 * nx, 3 * nx)] = jnp.zeros((3 * nx, nz), BF16)
-        up_ref[pl.ds(5 * nx, 16)] = jnp.zeros((16, nz), BF16)
-        down_ref[pl.ds(5 * nx, 16)] = jnp.zeros((16, nz), BF16)
 
     @pl.when(gy % 2 == 0)
     def _():
@@ -218,7 +226,7 @@
     def _():
         pack(yb_ref, ya_ref)
 
-    for one in extra[7:]:
+    for one in extra[7:] + faces(xa_ref, xb_ref):
         one.wait()
 
 
@@ -275,7 +283,7 @@
 
 def field_kernel(
     ef, hf, cf, xa_ref, xb_ref, ya_ref, yb_ref, y0_ref,
-    ne_hbm, nh_hbm,
+    ne_hbm, nh_hbm, fix_ref, tile_ref,
     ne, nh, gf, bz, high, beyond, esem, osem,
 ):
     gx, gy = lax.axis_index("gx"), lax.axis_index("gy")
@@ -309,22 +317,29 @@
     ex, ey, ez, hx, hz = [
         either(even_y, yb_ref[pl.ds(c * nx, nx)], ya_ref[pl.ds(c * nx, nx)]) for c in range(5)
     ]
-    corner = pl.ds(5 * nx, 16)
-    below, above = either(even_y, yb_ref[corner], ya_ref[corner]), either(even_y, ya_ref[corner], yb_ref[corner])
     inside = jnp.where(gy > 0, 1.0, 0.0)
     low_x = rounded(inside * (2.0 * hx - ((y0_ref[1] - ez) - (up_z(ey) - ey))))
-    low_z = rounded(inside * (2.0 * hz - ((up_row(ey, below[0:1]) - ey) - (y0_ref[0] - ex))))
+    low_z = rounded(inside * (2.0 * hz - ((up_row(ey, 0.0) - ey) - (y0_ref[0] - ex))))
     high[0] = either(even_y, ya_ref[pl.ds(0, nx)], yb_ref[pl.ds(0, nx)])
     high[1] = either(even_y, ya_ref[pl.ds(nx, nx)], yb_ref[pl.ds(nx, nx)])
     for x in range(nx):
         gf[0, x + 1, pl.ds(7, 1)] = low_x[x : x + 1]
         gf[2, x + 1, pl.ds(7, 1)] = low_z[x : x + 1]
+    far = slice(nx - 1, nx)
+    fix_ref[0:1] = 2.0 * hz[far]
+    fix_ref[1:2] = ey[far]
+    fix_ref[2:3] = y0_ref[0, pl.ds(nx - 1, 1)] - ex[far]
     for c in range(2):
         beyond[c] = either(even_x, xa_ref[c], xb_ref[c])
     ex, ey, ez, hy, hz = [either(even_x, xb_ref[c], xa_ref[c]) for c in range(5)]
     inside = jnp.where(gx > 0, 1.0, 0.0)
     gf[1, 0, kept] = rounded(inside * (2.0 * hy - ((up_z(ex) - ex) - (ef[2, 0, rows] - ez))))
-    gf[2, 0, kept] = rounded(inside * (2.0 * hz - ((ef[1, 0, rows] - ey) - (up_row(ex, above[0:1]) - ex))))
+    gf[2, 0, kept] = rounded(inside * (2.0 * hz - ((ef[1, 0, rows] - ey) - (up_row(ex, 0.0) - ex))))
+
+    far = slice(ny - 1, ny)
+    fix_ref[8:9] = 2.0 * hz[far]
+    fix_ref[9:10] = ef[1, 0, pl.ds(ny - 1, 1)] - ey[far]
+    fix_ref[10:11] = ex[far]
 
     back = 2.0 * (eye_like(0, nz) - eye_like(-1, nz))
     none = jnp.zeros((nz, nz), F32)
@@ -355,6 +370,14 @@
         ty = bz[0, slot] - (gz_ - gf[2, x, kept])
         tz = (gy_ - gf[1, x, kept]) - (gx_ - gf[0, x + 1, shifted])
         coef = cf[x]
+        if x == 0:
+            lines = (gz_[ny - 1 :], bz[0, slot][ny - 1 :], ef[1, 0, pl.ds(ny - 1, 1)], coef[ny - 1 :])
+            for k, line in enumerate(lines):
+                fix_ref[11 + k : 12 + k] = line
+        if x == nx - 1:
+            lines = (gz_[:1], bz[1, slot][:1], ef[0, x, pl.ds(0, 1)], coef[:1])
+            for k, line in enumerate(lines):
+                fix_ref[3 + k : 4 + k] = line
         for c, t in enumerate((tx, ty, tz)):
             ne[c, x] = (ef[c, x, rows] + coef * t).astype(BF16)
 
@@ -375,22 +398,57 @@
             stores[i][0].start()
         if i > 0:
             stores[i - 1][1].start()
+    tile_ref[0] = ne[0, nx - 1, pl.ds(0, 8)].astype(F32)
+    tile_ref[1] = ne[1, 0, pl.ds(ny - 8, 8)].astype(F32)
     for group in stores:
         for one in group:
             one.wait()
 
 
-def place_kernel(got_ref, grad_ref):
-    values = jnp.transpose(got_ref[pl.ds(0, 128, stride=2), :])
-    spots = got_ref[pl.ds(1, 128, stride=2), :].astype(I32)
+def place_kernel(sent_ref, fix_ref, tile_ref, _, grad_ref, ne_hbm, got_ref, tile, sem):
+    gx, gy = lax.axis_index("gx"), lax.axis_index("gy")
+    sx, sy = lax.axis_size("gx"), lax.axis_size("gy")
+    _, nx, ny, nz = ne_hbm.shape
+    got_ref[...] = sent_ref[...].astype(F32)
+
+    def corner(there, device):
+        line = got_ref[pl.ds(jnp.where(there, 4 * device + 3, 3), 1), :]
+        return jnp.where(there, line, 0.0)
+
+    def rounded(v):
+        return v.astype(BF16).astype(F32)
+
+    fix = [fix_ref[k : k + 1] for k in range(16)]
+    line = corner((gx < sx - 1) & (gy > 0), (gx + 1) * sy + gy - 1)
+    low = rounded(jnp.where(gy > 0, 1.0, 0.0) * (fix[0] - ((line - fix[1]) - fix[2])))
+    first = fix[5] + fix[6] * ((fix[3] - low) - fix[4])
+    line = corner((gx > 0) & (gy < sy - 1), (gx - 1) * sy + gy + 1)
+    low = rounded(jnp.where(gx > 0, 1.0, 0.0) * (fix[8] - (fix[9] - (line - fix[10]))))
+    second = fix[13] + fix[14] * (fix[12] - (fix[11] - low))
+    row = iota((8, nz), 0)
+    tile[0] = jnp.where(row == 0, first, tile_ref[0]).astype(BF16)
+    tile[1] = jnp.where(row == 7, second, tile_ref[1]).astype(BF16)
+    copies = [
+        pltpu.make_async_copy(tile.at[0], ne_hbm.at[0, nx - 1, pl.ds(0, 8)], sem.at[0]),
+        pltpu.make_async_copy(tile.at[1], ne_hbm.at[1, 0, pl.ds(ny - 8, 8)], sem.at[1]),
+    ]
+    for one in copies:
+        one.start()
+
+    upper = jnp.transpose(got_ref[pl.ds(0, 128, stride=4), :])
+    lower = jnp.transpose(got_ref[pl.ds(1, 128, stride=4), :])
+    spots = got_ref[pl.ds(2, 128, stride=4), :].astype(I32)
     spots = spots[:, :4] + spots[:, 4:8]
     ranks = grad_ref.shape[1]
     total = jnp.zeros((2 * DL, ranks), F32)
     for k in range(4):
         hot = jnp.where(iota((128, ranks), 1) == spots[:, k : k + 1], 1.0, 0.0).astype(BF16)
-        hi, lo = split(values[k * DL : (k + 1) * DL])
-        total = total + dot(jnp.concatenate([hi, lo], axis=0), hot)
+        part = slice(k * DL, (k + 1) * DL)
+        both = jnp.concatenate([upper[part], lower[part]], axis=0).astype(BF16)
+        total = total + dot(both, hot)
     grad_ref[...] = total[:DL] + total[DL:]
+    for one in copies:
+        one.wait()
 
 
 def per_device(
@@ -418,51 +476,38 @@
             pairs += [(i, i + 1), (i + 1, i)]
         return lax.ppermute(v, axis, pairs)
 
-    xa, xb = pl.pallas_call(
-        face_kernel,
-        out_shape=(shape((5, ny, nz), BF16), shape((5, ny, nz), BF16)),
-        in_specs=[HBM, HBM],
-        out_specs=[VM, VM],
-        scratch_shapes=[pltpu.SemaphoreType.DMA((3,))],
-        compiler_params=params(4),
-        name="faces",
-    )(adjoint_e, adjoint_h)
-    xa, xb = swap(xa, "gx", sx, 0), swap(xb, "gx", sx, 1)
-
-    send, ya, yb, y0, e_vm, m_vm = pl.pallas_call(
+    send, xa, xb, ya, yb, y0, e_vm, m_vm = pl.pallas_call(
         pillar_kernel,
         out_shape=(
-            shape((256, 128), F32),
-            shape((5 * nx + 16, nz), BF16), shape((5 * nx + 16, nz), BF16),
+            shape((512, 128), BF16),
+            shape((5, ny, nz), BF16), shape((5, ny, nz), BF16),
+            shape((5 * nx, nz), BF16), shape((5 * nx, nz), BF16),
             shape((2, nx, nz), F32),
             shape(adjoint_e.shape, BF16), shape((nx, ny, nz), I32),
         ),
         in_specs=[HBM] * 7,
-        out_specs=[VM] * 6,
+        out_specs=[VM] * 8,
         scratch_shapes=[
-            pltpu.VMEM((3, nx, ny, nz), BF16),
+            pltpu.VMEM((512, 128), F32), pltpu.VMEM((3, nx, ny, nz), BF16),
             pltpu.VMEM((3, nx, 8, nz), BF16), pltpu.VMEM((3, nx, 8, nz), BF16),
             pltpu.VMEM((2, nx, 8, nz), BF16),
             pltpu.VMEM((8, 512), I32), pltpu.VMEM((64, 128), I32), pltpu.VMEM((nx, ny), I32),
             pltpu.VMEM((nx, 2 * ny), I32), pltpu.VMEM((512, 128), I32),
             pltpu.VMEM((512, 2 * nz), F32),
             pltpu.SemaphoreType.DMA((PARTS,)), pltpu.SemaphoreType.DMA((PARTS,)),
-            pltpu.SemaphoreType.DMA((8,)),
+            pltpu.SemaphoreType.DMA((8,)), pltpu.SemaphoreType.DMA((3,)),
         ],
         compiler_params=params(12),
         name="pillars",
     )(adjoint_e, adjoint_h, material, forward_design, cell_slot, tile_pillars, ranks)
 
-    got = lax.all_to_all(send.reshape(128, 2, 128), both, 0, 0, tiled=True)
-    got = got.reshape(256, 128)
-
-    even_x, even_y = lax.axis_index("gx") % 2 == 0, lax.axis_index("gy") % 2 == 0
-    up = jnp.where(even_x, xa[0, ny - 1 :], xb[0, ny - 1 :])
-    down = jnp.where(even_x, xb[0, :1], xa[0, :1])
-    ya = lax.dynamic_update_slice(ya, jnp.where(even_y, up, down), (5 * nx, 0))
-    yb = lax.dynamic_update_slice(yb, jnp.where(even_y, down, up), (5 * nx, 0))
+    got = lax.all_to_all(send.reshape(128, 4, 128), both, 0, 0, tiled=True)
+    got = got.reshape(512, 128)
+
     ya = swap(ya, "gy", sy, 0)
     yb = swap(yb, "gy", sy, 1)
+    xa = swap(xa, "gx", sx, 0)
+    xb = swap(xb, "gx", sx, 1)
 
     ef, hf, cf = pl.pallas_call(
         spread_kernel,
@@ -476,11 +521,14 @@
         name="spread",
     )(e_vm, adjoint_h, m_vm, inv_eps)
 
-    new_e, new_h = pl.pallas_call(
+    new_e, new_h, fix, tiles = pl.pallas_call(
         field_kernel,
-        out_shape=(shape(adjoint_e.shape, BF16), shape(adjoint_e.shape, BF16)),
+        out_shape=(
+            shape(adjoint_e.shape, BF16), shape(adjoint_e.shape, BF16),
+            shape((16, nz), F32), shape((2, 8, nz), F32),
+        ),
         in_specs=[VM] * 8,
-        out_specs=[HBM, HBM],
+        out_specs=[HBM, HBM, VM, VM],
         scratch_shapes=[
             pltpu.VMEM((3, nx, ny, nz), BF16), pltpu.VMEM((3, nx, ny, nz), BF16),
             pltpu.VMEM((3, nx + 1, ny + 8, nz), F32),
@@ -491,14 +539,16 @@
         name="fields",
     )(ef, hf, cf, xa, xb, ya, yb, y0)
 
-    gradient = pl.pallas_call(
+    gradient, new_e = pl.pallas_call(
         place_kernel,
-        out_shape=shape((DL, 512), F32),
-        in_specs=[VM],
-        out_specs=VM,
+        out_shape=(shape((DL, 512), F32), shape(adjoint_e.shape, BF16)),
+        in_specs=[VM, VM, VM, HBM],
+        out_specs=[VM, HBM],
+        input_output_aliases={3: 1},
+        scratch_shapes=[pltpu.VMEM((512, 128), F32), pltpu.VMEM((2, 8, nz), BF16), pltpu.SemaphoreType.DMA((2,))],
         compiler_params=params(4),
         name="place",
-    )(got)
+    )(got, fix, tiles, new_e)
     return new_e, new_h, gradient
 
 

time: 32.5 us -> 34.4 us (1.058)
  the two profiles are of different devices: /device:TPU:1 before, /device:TPU:31 now
where the time goes in v5:
time: 34.4 us; the launch traced here: 34.2 us
  starting transfers between devices  20.1 us (58%)
  Pallas kernels  11 us (32%)
  waiting for transfers between devices  2.33 us (7%)
  between operations  0.71 us (2%)
    all_to_all x1, starting transfers between devices, per_device(): got = lax.all_to_all(send.reshape(128, 4, 128), both, 0, 0, tiled=True)  10.5 us
    ppermute x4, starting transfers between devices, swap(): return lax.ppermute(v, axis, pairs)  9.58 us
    pallas_call x1, Pallas kernels, per_device(): pl.pallas_call(pillar_kernel, out_shape=(shape((512, 128), BF16), shape((...  4.13 us
    pallas_call x1, Pallas kernels, per_device(): pl.pallas_call(spread_kernel, out_shape=(shape((3, nx, ny + 8, nz), F32),...  2.75 us
    pallas_call x1, Pallas kernels, per_device(): pl.pallas_call(field_kernel, out_shape=(shape(adjoint_e.shape, BF16), sha...  2.59 us
    ppermute x4, waiting for transfers between devices, swap(): return lax.ppermute(v, axis, pairs)  2.33 us
    pallas_call x1, Pallas kernels, per_device(): pl.pallas_call(place_kernel, out_shape=(shape((DL, 512), F32), shape(adjo...  1.55 us
  transfers between devices with their start and end apart: 5, of which 1 were waited for; matrix products, arithmetic and copies ran while one was open for 0% of the time, Pallas kernels for 16%

profile of v5, /device:TPU:31, one launch (start us, length us, event | category | flops | bytes accessed | tf_op | source)
XLA Modules:
  0.0 34.2 jit_solution(8198674314973154)
XLA Ops:
  0.6 0.0 copy-start
  0.6 4.1 %pillars.1 = (bf16[512,128]{1,0:T(8,128)(2,1)}, bf16[5,64,128]{2,1,0:T(8,128)(2,1)S(1)}, bf16[5,64,128]{2,1,0:T(8,128)(2,1)S(1)}, bf16[160,128]{1,0:T(8,128)(2,1...) custom-call(bf16[3,32,64,128]{3,2,1,0:T(8,128)(2,1)} %e_hbm.1, ...), custom_call_target="tpu_custom_call" | custom-call | tf_op jit(solution)/shard_map/pillars/pallas_call | solution.py:479
  4.8 10.5 %all-to-all-start = ((bf16[128,4,128]{2,1,0:T(4,128)(2,1)}), bf16[128,4,128]{2,1,0:T(4,128)(2,1)S(1)}, u32[]{:S(2)}, u32[]{:S(2)}) async-start(bf16[128,4,128]{2,1,0:T(4,128)(2,1)} %bitcast.1), calls=%async_computation | async-start | bytes 262144 | tf_op jit(solution)/shard_map/all_to_all | solution.py:504
  15.3 0.6 %collective-permute-start = (bf16[5,64,128]{2,1,0:T(8,128)(2,1)S(1)}, bf16[5,64,128]{2,1,0:T(8,128)(2,1)S(1)}, u32[]{:S(2)}, u32[]{:S(2)}) collective-permute-start(bf16[5,64,128]{2,1,0:T(8,128)(2,1)S(1)} %get-tuple-element.26), channel_id=1, source_target_pairs={{0,16},{16,0},{32,48},{48,32},{64,80},{80,64},{96,112},{112,96},{1... | collective-permute-start | bytes 245768 | tf_op jit(solution)/shard_map/ppermute | solution.py:477
  15.9 5.7 %collective-permute-start.1 = (bf16[5,64,128]{2,1,0:T(8,128)(2,1)S(1)}, bf16[5,64,128]{2,1,0:T(8,128)(2,1)S(1)}, u32[]{:S(2)}, u32[]{:S(2)}) collective-permute-start(bf16[5,64,128]{2,1,0:T(8,128)(2,1)S(1)} %get-tuple-element.27), channel_id=1, source_target_pairs={{16,32},{32,16},{48,64},{64,48},{80,96},{96,80},{17,33},{33,17},{4... | collective-permute-start | bytes 245768 | tf_op jit(solution)/shard_map/ppermute | solution.py:477
  21.6 1.0 %collective-permute-start.2 = (bf16[160,128]{1,0:T(8,128)(2,1)S(1)}, bf16[160,128]{1,0:T(8,128)(2,1)S(1)}, u32[]{:S(2)}, u32[]{:S(2)}) collective-permute-start(bf16[160,128]{1,0:T(8,128)(2,1)S(1)} %get-tuple-element.28), channel_id=1, source_target_pairs={{0,1},{1,0},{2,3},{3,2},{4,5},{5,4},{6,7},{7,6},{8,9},{9,8},{10,11... | collective-permute-start | bytes 122888 | tf_op jit(solution)/shard_map/ppermute | solution.py:477
  22.6 2.3 %collective-permute-start.3 = (bf16[160,128]{1,0:T(8,128)(2,1)S(1)}, bf16[160,128]{1,0:T(8,128)(2,1)S(1)}, u32[]{:S(2)}, u32[]{:S(2)}) collective-permute-start(bf16[160,128]{1,0:T(8,128)(2,1)S(1)} %get-tuple-element.29), channel_id=1, source_target_pairs={{1,2},{2,1},{3,4},{4,3},{5,6},{6,5},{7,8},{8,7},{9,10},{10,9},{11,... | collective-permute-start | bytes 122888 | tf_op jit(solution)/shard_map/ppermute | solution.py:477
  24.9 0.0 copy-done
  24.9 2.7 %spread.1 = (f32[3,32,72,128]{3,2,1,0:T(8,128)S(1)}, f32[3,32,64,128]{3,2,1,0:T(8,128)S(1)}, f32[32,64,128]{2,1,0:T(8,128)S(1)}) custom-call(bf16[3,32,64,128]{3,2,1,0:T(8,128)(2,1)S(1)} %get-tuple-element.21.e, bf16[3,32,64,128]{3,2,1,0:T(8,128)(2,1)} %h_hbm.3, s32[32,64,128]{2,1,0:T(8,128)S(1)} %get-tuple-element.22.m, f32[4]{0:T(128)S(1)} %copy-done), custom_call_target="tpu_custom_call" | custom-call | tf_op jit(solution)/shard_map/spread/pallas_call | solution.py:512
  27.7 0.0 collective-permute-done.2.ya_ref
  27.7 2.3 %collective-permute-done.3.yb_ref = bf16[160,128]{1,0:T(8,128)(2,1)S(1)} collective-permute-done((bf16[160,128]{1,0:T(8,128)(2,1)S(1)}, bf16[160,128]{1,0:T(8,128)(2,1)S(1)}, u32[]{:S(2)}, u32[]{:S(2)}) %collective-permute-start.3) | collective-permute-done | bytes 40992 | tf_op jit(solution)/shard_map/ppermute | solution.py:477
  30.0 0.0 collective-permute-done.xa_ref
  30.0 0.0 collective-permute-done.1.xb_ref
  30.0 2.6 %fields.1 = (bf16[3,32,64,128]{3,2,1,0:T(8,128)(2,1)}, bf16[3,32,64,128]{3,2,1,0:T(8,128)(2,1)}, f32[16,128]{1,0:T(8,128)S(1)}, f32[2,8,128]{2,1,0:T(8,128)S(1)}) custom-call(f32[3,32,72,128]{3,2,1,0:T(8,128)S(1)} %get-tuple-element.23.ef, f32[3,32,64,128]{3,2,1,0:T(8,128)S(1)} %get-tuple-element.24.hf, f32[32,64,128]{2,1,0:T(8,128)S(1)} %get-tuple-element.25.cf, ...), custom_call_target="tpu_custom_call" | custom-call | tf_op jit(solution)/shard_map/fields/pallas_call | solution.py:524
  32.6 0.0 all-to-all-done
  32.6 1.6 %place.1 = (f32[32,512]{1,0:T(8,128)}, bf16[3,32,64,128]{3,2,1,0:T(8,128)(2,1)}) custom-call(bf16[512,128]{1,0:T(8,128)(2,1)S(1)} %bitcast.3, f32[16,128]{1,0:T(8,128)S(1)} %get-tuple-element.31.fix_ref, f32[2,8,128]{2,1,0:T(8,128)S(1)} %get-tuple-element.32.tile_ref, bf16[3,32,64,128]{3,2,1,0:T(8,128)(2,1)} %get-tuple-element.33._), custom_call_target="tpu_custom_call", output_to_operand_aliasing={{1}: (3, {})} | custom-call | tf_op jit(solution)/shard_map/place/pallas_call | solution.py:542
Async XLA Ops:
  0.6 24.3 %copy-start = (f32[4]{0:T(128)S(1)}, f32[4]{0:T(128)}, u32[]{:S(2)}) copy-start(f32[4]{0:T(128)} %eps_ref.1) | copy-start | bytes 52
  4.8 27.8 %all-to-all-start = ((bf16[128,4,128]{2,1,0:T(4,128)(2,1)}), bf16[128,4,128]{2,1,0:T(4,128)(2,1)S(1)}, u32[]{:S(2)}, u32[]{:S(2)}) async-start(bf16[128,4,128]{2,1,0:T(4,128)(2,1)} %bitcast.1), calls=%async_computation | async-start | bytes 262144 | tf_op jit(solution)/shard_map/all_to_all | solution.py:504
  15.3 14.7 %collective-permute-start = (bf16[5,64,128]{2,1,0:T(8,128)(2,1)S(1)}, bf16[5,64,128]{2,1,0:T(8,128)(2,1)S(1)}, u32[]{:S(2)}, u32[]{:S(2)}) collective-permute-start(bf16[5,64,128]{2,1,0:T(8,128)(2,1)S(1)} %get-tuple-element.26), channel_id=1, source_target_pairs={{0,16},{16,0},{32,48},{48,32},{64,80},{80,64},{96,112},{112,96},{1... | collective-permute-start | bytes 245768 | tf_op jit(solution)/shard_map/ppermute | solution.py:477
  15.9 14.1 %collective-permute-start.1 = (bf16[5,64,128]{2,1,0:T(8,128)(2,1)S(1)}, bf16[5,64,128]{2,1,0:T(8,128)(2,1)S(1)}, u32[]{:S(2)}, u32[]{:S(2)}) collective-permute-start(bf16[5,64,128]{2,1,0:T(8,128)(2,1)S(1)} %get-tuple-element.27), channel_id=1, source_target_pairs={{16,32},{32,16},{48,64},{64,48},{80,96},{96,80},{17,33},{33,17},{4... | collective-permute-start | bytes 245768 | tf_op jit(solution)/shard_map/ppermute | solution.py:477
  21.6 6.1 %collective-permute-start.2 = (bf16[160,128]{1,0:T(8,128)(2,1)S(1)}, bf16[160,128]{1,0:T(8,128)(2,1)S(1)}, u32[]{:S(2)}, u32[]{:S(2)}) collective-permute-start(bf16[160,128]{1,0:T(8,128)(2,1)S(1)} %get-tuple-element.28), channel_id=1, source_target_pairs={{0,1},{1,0},{2,3},{3,2},{4,5},{5,4},{6,7},{7,6},{8,9},{9,8},{10,11... | collective-permute-start | bytes 122888 | tf_op jit(solution)/shard_map/ppermute | solution.py:477
  22.6 7.4 %collective-permute-start.3 = (bf16[160,128]{1,0:T(8,128)(2,1)S(1)}, bf16[160,128]{1,0:T(8,128)(2,1)S(1)}, u32[]{:S(2)}, u32[]{:S(2)}) collective-permute-start(bf16[160,128]{1,0:T(8,128)(2,1)S(1)} %get-tuple-element.29), channel_id=1, source_target_pairs={{1,2},{2,1},{3,4},{4,3},{5,6},{6,5},{7,8},{8,7},{9,10},{10,9},{11,... | collective-permute-start | bytes 122888 | tf_op jit(solution)/shard_map/ppermute | solution.py:477

commit v6 on v5

--- a/solution.py
+++ b/solution.py
@@ -39,8 +39,8 @@
 
 def pillar_kernel(
     e_hbm, h_hbm, m_hbm, f_hbm, slot_hbm, tiles_hbm, rank_hbm,
-    sent_ref, xa_ref, xb_ref, ya_ref, yb_ref, y0_ref, e, m,
-    send_ref, f, y_first, y_last, y_h, tiles, rank, slot, cells, ids, acc, sem, fsem, msem, xsem,
+    sent_ref, xa_ref, xb_ref, ya_ref, yb_ref, y0_ref, e, hxy, kinds,
+    send_ref, m, f, y_h, tiles, rank, slot, cells, ids, acc, sem, fsem, msem, xsem,
 ):
     gx, gy = lax.axis_index("gx"), lax.axis_index("gy")
     _, nx, ny, nz = e.shape
@@ -57,11 +57,10 @@
         pltpu.make_async_copy(tiles_hbm.at[gx, pl.ds(gy // 8 * 8, 8)], tiles, msem.at[0]),
         pltpu.make_async_copy(rank_hbm.at[pl.ds(gx * 64, 64)], rank, msem.at[1]),
         pltpu.make_async_copy(slot_hbm, slot, msem.at[2]),
-        pltpu.make_async_copy(e_hbm.at[:, :, pl.ds(0, 8)], y_first, msem.at[3]),
-        pltpu.make_async_copy(e_hbm.at[:, :, pl.ds(ny - 8, 8)], y_last, msem.at[4]),
-        pltpu.make_async_copy(h_hbm.at[0, :, pl.ds(ny - 8, 8)], y_h.at[0], msem.at[5]),
-        pltpu.make_async_copy(h_hbm.at[2, :, pl.ds(ny - 8, 8)], y_h.at[1], msem.at[6]),
-        pltpu.make_async_copy(m_hbm, m, msem.at[7]),
+        pltpu.make_async_copy(h_hbm.at[0, :, pl.ds(ny - 8, 8)], y_h.at[0], msem.at[3]),
+        pltpu.make_async_copy(h_hbm.at[2, :, pl.ds(ny - 8, 8)], y_h.at[1], msem.at[4]),
+        pltpu.make_async_copy(m_hbm, m, msem.at[5]),
+        pltpu.make_async_copy(h_hbm.at[pl.ds(0, 2)], hxy, msem.at[6]),
     ]
     for one in extra[:3]:
         one.start()
@@ -182,8 +181,9 @@
     send_ref[pl.ds(0, 128, stride=4), :] = hi.astype(F32)
     send_ref[pl.ds(1, 128, stride=4), :] = lo.astype(F32)
 
-    for one in extra[3:7]:
+    for one in extra[3:5]:
         one.wait()
+    tops, ends = pl.ds(0, 8), pl.ds(ny - 8, 8)
     at = iota((nx, 8 * nx), 1) - 8 * iota((nx, 8 * nx), 0)
     low = jnp.where(at == 0, 1.0, 0.0).astype(BF16)
     high = jnp.where(at == 7, 1.0, 0.0).astype(BF16)
@@ -193,8 +193,8 @@
         both = dot(which, both)
         return both[:, :nz], both[:, nz:]
 
-    y0x, y0z = face(low, y_first[0], y_first[2])
-    up_y = face(high, y_last[0], y_last[1]) + face(high, y_last[2], y_h[0]) + face(high, y_h[1], y_h[1])[:1]
+    y0x, y0z = face(low, e[0, :, tops, :], e[2, :, tops, :])
+    up_y = face(high, e[0, :, ends, :], e[1, :, ends, :]) + face(high, e[2, :, ends, :], y_h[0]) + face(high, y_h[1], y_h[1])[:1]
     y0_ref[0] = y0x
     y0_ref[1] = y0z
 
@@ -226,7 +226,13 @@
     def _():
         pack(yb_ref, ya_ref)
 
-    for one in extra[7:] + faces(xa_ref, xb_ref):
+    extra[5].wait()
+    for p in range(nx // 16):
+        packed = m[16 * p]
+        for k in range(1, 16):
+            packed = packed | (m[16 * p + k] << (2 * k))
+        kinds[p] = packed
+    for one in extra[6:] + faces(xa_ref, xb_ref):
         one.wait()
 
 
@@ -244,32 +250,21 @@
     return jnp.concatenate([one.reshape(shape), two.reshape(shape)], axis=1)
 
 
-def spread_kernel(e, h_hbm, m, eps_ref, ef_ref, hf_ref, cf_ref, h, sem):
-    nx, ny, nz = m.shape
+def spread_kernel(e, hxy, kinds, h_hbm, eps_ref, ef_ref, hf_ref, cf_ref, hz, sem):
+    _, nx, ny, nz = e.shape
     step = nx // PARTS
-    loads = []
-    for i in range(PARTS):
-        part = pl.ds(i * step, step)
-        loads.append(pltpu.make_async_copy(h_hbm.at[:, part], h.at[:, part], sem.at[i]))
-    for one in loads:
-        one.start()
+    load = pltpu.make_async_copy(h_hbm.at[2], hz, sem)
+    load.start()
     values = [0.25 * eps_ref[k] for k in range(4)]
     eye = eye_like(0, nz)
     ahead = eye_like(1, nz) - eye
     none = jnp.zeros((nz, nz), F32)
     wx = square(2.0 * eye, none, ahead, eye)
     wy = square(2.0 * eye, none, -ahead, eye)
-    for x in range(nx):
-        kind = m[x]
-        cf_ref[x] = jnp.where(
-            kind < 2, jnp.where(kind == 0, values[0], values[1]), jnp.where(kind == 2, values[2], values[3])
-        )
-        ef_ref[2, x, pl.ds(0, ny)] = e[2, x].astype(F32)
     for i in range(PARTS):
-        loads[i].wait()
         part = pl.ds(i * step, step)
         for c, other, w in ((0, 1, wx), (1, 0, wy)):
-            both = dot(side(h[c, part], e[other, part]), w)
+            both = dot(side(hxy[c, part], e[other, part]), w)
             for k in range(step):
                 x = i * step + k
                 line = both[k * ny : (k + 1) * ny]
@@ -277,8 +272,15 @@
                 ef_ref[other, x, pl.ds(0, ny)] = line[:, nz:]
         for k in range(step):
             x = i * step + k
-            hz = h[2, x].astype(F32)
-            hf_ref[2, x] = hz + hz
+            kind = (kinds[x // 16] >> (2 * (x % 16))) & 3
+            cf_ref[x] = jnp.where(
+                kind < 2, jnp.where(kind == 0, values[0], values[1]), jnp.where(kind == 2, values[2], values[3])
+            )
+            ef_ref[2, x, pl.ds(0, ny)] = e[2, x].astype(F32)
+    load.wait()
+    for x in range(nx):
+        line = hz[x].astype(F32)
+        hf_ref[2, x] = line + line
 
 
 def field_kernel(
@@ -435,17 +437,14 @@
     for one in copies:
         one.start()
 
-    upper = jnp.transpose(got_ref[pl.ds(0, 128, stride=4), :])
-    lower = jnp.transpose(got_ref[pl.ds(1, 128, stride=4), :])
+    values = jnp.transpose(got_ref[pl.ds(0, 128, stride=4), :] + got_ref[pl.ds(1, 128, stride=4), :])
     spots = got_ref[pl.ds(2, 128, stride=4), :].astype(I32)
     spots = spots[:, :4] + spots[:, 4:8]
     ranks = grad_ref.shape[1]
     total = jnp.zeros((2 * DL, ranks), F32)
     for k in range(4):
         hot = jnp.where(iota((128, ranks), 1) == spots[:, k : k + 1], 1.0, 0.0).astype(BF16)
-        part = slice(k * DL, (k + 1) * DL)
-        both = jnp.concatenate([upper[part], lower[part]], axis=0).astype(BF16)
-        total = total + dot(both, hot)
+        total = total + dot(jnp.concatenate(split(values[k * DL : (k + 1) * DL]), axis=0), hot)
     grad_ref[...] = total[:DL] + total[DL:]
     for one in copies:
         one.wait()
@@ -476,28 +475,28 @@
             pairs += [(i, i + 1), (i + 1, i)]
         return lax.ppermute(v, axis, pairs)
 
-    send, xa, xb, ya, yb, y0, e_vm, m_vm = pl.pallas_call(
+    send, xa, xb, ya, yb, y0, e_vm, h_vm, kinds = pl.pallas_call(
         pillar_kernel,
         out_shape=(
             shape((512, 128), BF16),
             shape((5, ny, nz), BF16), shape((5, ny, nz), BF16),
             shape((5 * nx, nz), BF16), shape((5 * nx, nz), BF16),
             shape((2, nx, nz), F32),
-            shape(adjoint_e.shape, BF16), shape((nx, ny, nz), I32),
+            shape(adjoint_e.shape, BF16), shape((2, nx, ny, nz), BF16), shape((nx // 16, ny, nz), I32),
         ),
         in_specs=[HBM] * 7,
-        out_specs=[VM] * 8,
+        out_specs=[VM] * 9,
         scratch_shapes=[
-            pltpu.VMEM((512, 128), F32), pltpu.VMEM((3, nx, ny, nz), BF16),
-            pltpu.VMEM((3, nx, 8, nz), BF16), pltpu.VMEM((3, nx, 8, nz), BF16),
+            pltpu.VMEM((512, 128), F32), pltpu.VMEM((nx, ny, nz), I32),
+            pltpu.VMEM((3, nx, ny, nz), BF16),
             pltpu.VMEM((2, nx, 8, nz), BF16),
             pltpu.VMEM((8, 512), I32), pltpu.VMEM((64, 128), I32), pltpu.VMEM((nx, ny), I32),
             pltpu.VMEM((nx, 2 * ny), I32), pltpu.VMEM((512, 128), I32),
             pltpu.VMEM((512, 2 * nz), F32),
             pltpu.SemaphoreType.DMA((PARTS,)), pltpu.SemaphoreType.DMA((PARTS,)),
-            pltpu.SemaphoreType.DMA((8,)), pltpu.SemaphoreType.DMA((3,)),
+            pltpu.SemaphoreType.DMA((7,)), pltpu.SemaphoreType.DMA((3,)),
         ],
-        compiler_params=params(12),
+        compiler_params=params(14),
         name="pillars",
     )(adjoint_e, adjoint_h, material, forward_design, cell_slot, tile_pillars, ranks)
 
@@ -514,12 +513,12 @@
         out_shape=(
             shape((3, nx, ny + 8, nz), F32), shape((3, nx, ny, nz), F32), shape((nx, ny, nz), F32)
         ),
-        in_specs=[VM, HBM, VM, SM],
+        in_specs=[VM, VM, VM, HBM, SM],
         out_specs=[VM] * 3,
-        scratch_shapes=[pltpu.VMEM((3, nx, ny, nz), BF16), pltpu.SemaphoreType.DMA((PARTS,))],
+        scratch_shapes=[pltpu.VMEM((nx, ny, nz), BF16), pltpu.SemaphoreType.DMA],
         compiler_params=params(16),
         name="spread",
-    )(e_vm, adjoint_h, m_vm, inv_eps)
+    )(e_vm, h_vm, kinds, adjoint_h, inv_eps)
 
     new_e, new_h, fix, tiles = pl.pallas_call(
         field_kernel,

time: 34.4 us -> 34.5 us (level)
  waiting for transfers between devices: 2.33 us -> 3.39 us
  Pallas kernels: 11 us -> 10 us
    ppermute x4, waiting for transfers between devices: 2.33 us -> 3.39 us  [swap(): return lax.ppermute(v, axis, pairs)]
    pallas_call x1, Pallas kernels: 2.75 us -> 1.69 us  [per_device(): pl.pallas_call(spread_kernel, out_shape=(shape((3, nx, ny + 8, nz), F32),...]
  transfers between devices with their start and end apart: 5 -> 5, of which waited for: 1 -> 1; matrix products, arithmetic and copies ran while one was open for 0% -> 0% of each run, Pallas kernels for 16% -> 12%
where the time goes in v6:
time: 34.5 us; the launch traced here: 34.3 us
  starting transfers between devices  20.1 us (58%)
  Pallas kernels  10 us (29%)
  waiting for transfers between devices  3.39 us (10%)
  between operations  0.71 us (2%)
    all_to_all x1, starting transfers between devices, per_device(): got = lax.all_to_all(send.reshape(128, 4, 128), both, 0, 0, tiled=True)  10.5 us
    ppermute x4, starting transfers between devices, swap(): return lax.ppermute(v, axis, pairs)  9.58 us
    pallas_call x1, Pallas kernels, per_device(): pl.pallas_call(pillar_kernel, out_shape=(shape((512, 128), BF16), shape((...  4.2 us
    ppermute x4, waiting for transfers between devices, swap(): return lax.ppermute(v, axis, pairs)  3.39 us
    pallas_call x1, Pallas kernels, per_device(): pl.pallas_call(field_kernel, out_shape=(shape(adjoint_e.shape, BF16), sha...  2.59 us
    pallas_call x1, Pallas kernels, per_device(): pl.pallas_call(spread_kernel, out_shape=(shape((3, nx, ny + 8, nz), F32),...  1.69 us
    pallas_call x1, Pallas kernels, per_device(): pl.pallas_call(place_kernel, out_shape=(shape((DL, 512), F32), shape(adjo...  1.55 us
  transfers between devices with their start and end apart: 5, of which 1 were waited for; matrix products, arithmetic and copies ran while one was open for 0% of the time, Pallas kernels for 12%

profile of v6, /device:TPU:31, one launch (start us, length us, event | category | flops | bytes accessed | tf_op | source)
XLA Modules:
  0.0 34.3 jit_solution(5577777168160788739)
XLA Ops:
  0.6 0.0 copy-start
  0.6 4.2 %pillars.1 = (bf16[512,128]{1,0:T(8,128)(2,1)}, bf16[5,64,128]{2,1,0:T(8,128)(2,1)S(1)}, bf16[5,64,128]{2,1,0:T(8,128)(2,1)S(1)}, bf16[160,128]{1,0:T(8,128)(2,1...) custom-call(bf16[3,32,64,128]{3,2,1,0:T(8,128)(2,1)} %e_hbm.1, ...), custom_call_target="tpu_custom_call" | custom-call | tf_op jit(solution)/shard_map/pillars/pallas_call | solution.py:478
  4.8 10.5 %all-to-all-start = ((bf16[128,4,128]{2,1,0:T(4,128)(2,1)}), bf16[128,4,128]{2,1,0:T(4,128)(2,1)S(1)}, u32[]{:S(2)}, u32[]{:S(2)}) async-start(bf16[128,4,128]{2,1,0:T(4,128)(2,1)} %bitcast.1), calls=%async_computation | async-start | bytes 262144 | tf_op jit(solution)/shard_map/all_to_all | solution.py:503
  15.4 0.6 %collective-permute-start = (bf16[5,64,128]{2,1,0:T(8,128)(2,1)S(1)}, bf16[5,64,128]{2,1,0:T(8,128)(2,1)S(1)}, u32[]{:S(2)}, u32[]{:S(2)}) collective-permute-start(bf16[5,64,128]{2,1,0:T(8,128)(2,1)S(1)} %get-tuple-element.28), channel_id=1, source_target_pairs={{0,16},{16,0},{32,48},{48,32},{64,80},{80,64},{96,112},{112,96},{1... | collective-permute-start | bytes 245768 | tf_op jit(solution)/shard_map/ppermute | solution.py:476
  16.0 5.7 %collective-permute-start.1 = (bf16[5,64,128]{2,1,0:T(8,128)(2,1)S(1)}, bf16[5,64,128]{2,1,0:T(8,128)(2,1)S(1)}, u32[]{:S(2)}, u32[]{:S(2)}) collective-permute-start(bf16[5,64,128]{2,1,0:T(8,128)(2,1)S(1)} %get-tuple-element.29), channel_id=1, source_target_pairs={{16,32},{32,16},{48,64},{64,48},{80,96},{96,80},{17,33},{33,17},{4... | collective-permute-start | bytes 245768 | tf_op jit(solution)/shard_map/ppermute | solution.py:476
  21.6 1.0 %collective-permute-start.2 = (bf16[160,128]{1,0:T(8,128)(2,1)S(1)}, bf16[160,128]{1,0:T(8,128)(2,1)S(1)}, u32[]{:S(2)}, u32[]{:S(2)}) collective-permute-start(bf16[160,128]{1,0:T(8,128)(2,1)S(1)} %get-tuple-element.30), channel_id=1, source_target_pairs={{0,1},{1,0},{2,3},{3,2},{4,5},{5,4},{6,7},{7,6},{8,9},{9,8},{10,11... | collective-permute-start | bytes 122888 | tf_op jit(solution)/shard_map/ppermute | solution.py:476
  22.7 2.3 %collective-permute-start.3 = (bf16[160,128]{1,0:T(8,128)(2,1)S(1)}, bf16[160,128]{1,0:T(8,128)(2,1)S(1)}, u32[]{:S(2)}, u32[]{:S(2)}) collective-permute-start(bf16[160,128]{1,0:T(8,128)(2,1)S(1)} %get-tuple-element.31), channel_id=1, source_target_pairs={{1,2},{2,1},{3,4},{4,3},{5,6},{6,5},{7,8},{8,7},{9,10},{10,9},{11,... | collective-permute-start | bytes 122888 | tf_op jit(solution)/shard_map/ppermute | solution.py:476
  25.0 0.0 copy-done
  25.0 1.7 %spread.1 = (f32[3,32,72,128]{3,2,1,0:T(8,128)S(1)}, f32[3,32,64,128]{3,2,1,0:T(8,128)S(1)}, f32[32,64,128]{2,1,0:T(8,128)S(1)}) custom-call(bf16[3,32,64,128]{3,2,1,0:T(8,128)(2,1)S(1)} %get-tuple-element.22.e, bf16[2,32,64,128]{3,2,1,0:T(8,128)(2,1)S(1)} %get-tuple-element.23.hxy, s32[2,64,128]{2,1,0:T(8,128)S(1)} %get-tuple-element.24.kinds, ...), custom_call_target="tpu_custom_call" | custom-call | tf_op jit(solution)/shard_map/spread/pallas_call | solution.py:511
  26.7 0.0 collective-permute-done.2.ya_ref
  26.7 3.4 %collective-permute-done.3.yb_ref = bf16[160,128]{1,0:T(8,128)(2,1)S(1)} collective-permute-done((bf16[160,128]{1,0:T(8,128)(2,1)S(1)}, bf16[160,128]{1,0:T(8,128)(2,1)S(1)}, u32[]{:S(2)}, u32[]{:S(2)}) %collective-permute-start.3) | collective-permute-done | bytes 40992 | tf_op jit(solution)/shard_map/ppermute | solution.py:476
  30.1 0.0 collective-permute-done.xa_ref
  30.1 0.0 collective-permute-done.1.xb_ref
  30.1 2.6 %fields.1 = (bf16[3,32,64,128]{3,2,1,0:T(8,128)(2,1)}, bf16[3,32,64,128]{3,2,1,0:T(8,128)(2,1)}, f32[16,128]{1,0:T(8,128)S(1)}, f32[2,8,128]{2,1,0:T(8,128)S(1)}) custom-call(f32[3,32,72,128]{3,2,1,0:T(8,128)S(1)} %get-tuple-element.25.ef, f32[3,32,64,128]{3,2,1,0:T(8,128)S(1)} %get-tuple-element.26.hf, f32[32,64,128]{2,1,0:T(8,128)S(1)} %get-tuple-element.27.cf, ...), custom_call_target="tpu_custom_call" | custom-call | tf_op jit(solution)/shard_map/fields/pallas_call | solution.py:523
  32.7 0.0 all-to-all-done
  32.7 1.6 %place.1 = (f32[32,512]{1,0:T(8,128)}, bf16[3,32,64,128]{3,2,1,0:T(8,128)(2,1)}) custom-call(bf16[512,128]{1,0:T(8,128)(2,1)S(1)} %bitcast.3, f32[16,128]{1,0:T(8,128)S(1)} %get-tuple-element.33.fix_ref, f32[2,8,128]{2,1,0:T(8,128)S(1)} %get-tuple-element.34.tile_ref, bf16[3,32,64,128]{3,2,1,0:T(8,128)(2,1)} %get-tuple-element.35._), custom_call_target="tpu_custom_call", output_to_operand_aliasing={{1}: (3, {})} | custom-call | tf_op jit(solution)/shard_map/place/pallas_call | solution.py:541
Async XLA Ops:
  0.6 24.4 %copy-start = (f32[4]{0:T(128)S(1)}, f32[4]{0:T(128)}, u32[]{:S(2)}) copy-start(f32[4]{0:T(128)} %eps_ref.1) | copy-start | bytes 52
  4.8 27.8 %all-to-all-start = ((bf16[128,4,128]{2,1,0:T(4,128)(2,1)}), bf16[128,4,128]{2,1,0:T(4,128)(2,1)S(1)}, u32[]{:S(2)}, u32[]{:S(2)}) async-start(bf16[128,4,128]{2,1,0:T(4,128)(2,1)} %bitcast.1), calls=%async_computation | async-start | bytes 262144 | tf_op jit(solution)/shard_map/all_to_all | solution.py:503
  15.4 14.7 %collective-permute-start = (bf16[5,64,128]{2,1,0:T(8,128)(2,1)S(1)}, bf16[5,64,128]{2,1,0:T(8,128)(2,1)S(1)}, u32[]{:S(2)}, u32[]{:S(2)}) collective-permute-start(bf16[5,64,128]{2,1,0:T(8,128)(2,1)S(1)} %get-tuple-element.28), channel_id=1, source_target_pairs={{0,16},{16,0},{32,48},{48,32},{64,80},{80,64},{96,112},{112,96},{1... | collective-permute-start | bytes 245768 | tf_op jit(solution)/shard_map/ppermute | solution.py:476
  16.0 14.1 %collective-permute-start.1 = (bf16[5,64,128]{2,1,0:T(8,128)(2,1)S(1)}, bf16[5,64,128]{2,1,0:T(8,128)(2,1)S(1)}, u32[]{:S(2)}, u32[]{:S(2)}) collective-permute-start(bf16[5,64,128]{2,1,0:T(8,128)(2,1)S(1)} %get-tuple-element.29), channel_id=1, source_target_pairs={{16,32},{32,16},{48,64},{64,48},{80,96},{96,80},{17,33},{33,17},{4... | collective-permute-start | bytes 245768 | tf_op jit(solution)/shard_map/ppermute | solution.py:476
  21.6 5.1 %collective-permute-start.2 = (bf16[160,128]{1,0:T(8,128)(2,1)S(1)}, bf16[160,128]{1,0:T(8,128)(2,1)S(1)}, u32[]{:S(2)}, u32[]{:S(2)}) collective-permute-start(bf16[160,128]{1,0:T(8,128)(2,1)S(1)} %get-tuple-element.30), channel_id=1, source_target_pairs={{0,1},{1,0},{2,3},{3,2},{4,5},{5,4},{6,7},{7,6},{8,9},{9,8},{10,11... | collective-permute-start | bytes 122888 | tf_op jit(solution)/shard_map/ppermute | solution.py:476
  22.7 7.4 %collective-permute-start.3 = (bf16[160,128]{1,0:T(8,128)(2,1)S(1)}, bf16[160,128]{1,0:T(8,128)(2,1)S(1)}, u32[]{:S(2)}, u32[]{:S(2)}) collective-permute-start(bf16[160,128]{1,0:T(8,128)(2,1)S(1)} %get-tuple-element.31), channel_id=1, source_target_pairs={{1,2},{2,1},{3,4},{4,3},{5,6},{6,5},{7,8},{8,7},{9,10},{10,9},{11,... | collective-permute-start | bytes 122888 | tf_op jit(solution)/shard_map/ppermute | solution.py:476
